TPU v7x, 256 devices: a whole 4x4x8 slice. The times are simulated.
256 devices in a mesh: level: 2 (over core), group: 32 (over y, z), leaf: 4 (over x).
Axes of the slice: x: 4, y: 4, z: 8, core: 2. Of those that a mesh axis runs over, the one named last changes fastest.
Arguments:
- queries: bfloat16 [3072, 2048], P('group'), may hold values from -6 to 6
- weights: bfloat16 [2, 4, 32, 2048, 1024], P('level', 'leaf', 'group'), may hold values from -0.125 to 0.125
- block_mask: int32 [2, 4, 32, 16], P('level', 'leaf', 'group'), may hold values 0 or 1
- label_map: int32 [2, 4, 32, 1024], P('level', 'leaf', 'group'), may hold values from 0 to 1023, each once within a row
- beam_lists: int32 [2, 3072, 4], P('level', 'group'), may hold values from 0 to 31, all different within a row; in each aligned block of 32 rows (0 to 31, 32 to 63, ..., all dimensions but the last counted through in order) at most 8 rows name the same one
- root_score: bfloat16 [3072, 4], P('group'), may hold values from 0.19921875 to 1
- parent_pos: int32 [3072, 4], P('group'), may hold values from 0 to 4095
Outputs:
- scores: float32 [2, 3072, 4, 1024], P('level', 'group', None, 'leaf')
Inputs may be any that keep to these rules, and one draw needn't show every extreme that they name: `beam_lists`: each row names 4 different groups; in each aligned block of 32 rows (both levels' rows taken in order) no group is named by more than 8 rows, a bound that some block reaches. `label_map`: each row is a permutation of 0 to 1023.
All inputs are finite; a program needn't handle non-finite values. No bound on the sum of `block_mask` on one device may be relied on, other than what follows from the above.
Results may differ from a plain program's by a relative error of at most 0.0013.
Values may be sent and summed in bfloat16 or wider, within the bound.
A program may use at most 128 MiB of HBM per device.

v0:
```python
import jax
import jax.numpy as jnp
from jax import lax
from jax.sharding import PartitionSpec as P

QBLK = 32


def cut_along(value, dim, peers):
    before, after = (value.shape[:dim], value.shape[dim + 1 :])
    return jnp.moveaxis(value.reshape(*before, peers, -1, *after), dim, 0)


def sent_and_summed(value, axis, dim):
    peers = lax.axis_size(axis)
    pieces = lax.all_to_all(cut_along(value, dim, peers), axis, 0, 0, tiled=True)
    return jnp.sum(pieces, axis=0)


def sent_to_all(value, axis):
    peers = lax.axis_size(axis)
    return lax.all_to_all(
        jnp.broadcast_to(value[None], (peers, *value.shape)), axis, 0, 0, tiled=True
    )


def of_everyone(value, axis):
    everything = sent_to_all(value, axis)
    return jnp.sum(everything, axis=0)


def passed_along(block, axis, distance):
    devices = range(lax.axis_size(axis))
    route = [(i - distance, i) for i in devices if i - distance in devices]
    return lax.ppermute(block, axis, route)


def body(queries, weights, block_mask, label_map, beam_lists, root_score, parent_pos):
    group_count = lax.axis_size("group")
    leaf_count = lax.axis_size("leaf")
    section_index = lax.axis_index("level")
    leaf_index = lax.axis_index("leaf")
    local_blocks = weights.shape[2]
    feature = weights.shape[3]
    label_width = weights.shape[4]
    share_width = label_width // leaf_count
    beam_len = beam_lists.shape[2]
    all_rows = queries.shape[0]
    groups = local_blocks * group_count
    capacity = min(QBLK, max(2, 2 * QBLK * beam_len // groups))
    keeping = jnp.repeat(block_mask[0, 0], feature // block_mask.shape[3], axis=1).astype(
        weights.dtype
    )
    scorer = weights[0, 0]
    column_map = label_map[0, 0]
    block_cap = all_rows // QBLK * capacity
    slot_count = groups * block_cap
    entries = all_rows * beam_len
    unit_parent = jnp.ones((all_rows, beam_len), jnp.bfloat16)
    beam_block = beam_lists[0]
    group_of = beam_block.reshape(-1)
    onehot = (group_of[:, None] == jnp.arange(groups, dtype=jnp.int32)[None, :]).astype(jnp.int32)
    before = jnp.cumsum(onehot, axis=0) - onehot
    slot_rank = jnp.sum(before * onehot, axis=1)
    slot_of = group_of * block_cap + slot_rank
    source = (
        jnp.full((slot_count,), entries, jnp.int32)
        .at[slot_of]
        .set(jnp.arange(entries, dtype=jnp.int32))
    )
    filled = source < entries
    picked_entry = jnp.minimum(source, entries - 1)
    routed = jnp.take(queries, picked_entry // beam_len, axis=0) * filled[:, None].astype(
        jnp.bfloat16
    )
    routed_parent = jnp.take(unit_parent.reshape(-1), picked_entry) * filled.astype(jnp.bfloat16)
    routed = routed.reshape(group_count, local_blocks, block_cap, feature)
    routed_parent = routed_parent.reshape(group_count, local_blocks, block_cap)

    def compute(operands):
        kept_rows = operands[0] * keeping[None, :, None, :]
        logits = jnp.einsum("sjcd,jdl->sjcl", kept_rows, scorer, preferred_element_type=jnp.float32)
        logits = jnp.take_along_axis(logits, column_map[None, :, None, :], axis=3)
        return jax.nn.sigmoid(logits) * operands[1][..., None].astype(jnp.float32)

    def skipped(operands):
        return jnp.zeros(operands[0].shape[:3] + (label_width,), jnp.float32)

    scored = lax.cond(
        True,
        compute,
        skipped,
        (
            lax.all_to_all(routed, "group", split_axis=0, concat_axis=0, tiled=True),
            lax.all_to_all(routed_parent, "group", split_axis=0, concat_axis=0, tiled=True),
        ),
    )
    summed = sent_and_summed(scored, "leaf", 3)
    returning = lax.all_to_all(summed, "group", split_axis=0, concat_axis=0, tiled=True)
    returned = returning
    returned = returned.reshape(slot_count, returned.shape[3])
    gathered = jnp.take(returned, slot_of, axis=0).reshape(all_rows, beam_len, returned.shape[1])
    first_scaled = gathered * root_score.astype(jnp.float32)[..., None]
    row_count = first_scaled.shape[0]
    slot_pick = parent_pos // label_width
    label_pick = parent_pos % label_width - leaf_index * share_width
    inside = (label_pick >= 0) & (label_pick < share_width)
    flat_share = first_scaled.reshape(row_count, beam_len * share_width)
    pick_at = slot_pick * share_width + jnp.clip(label_pick, 0, share_width - 1)
    local_pick = jnp.take_along_axis(flat_share, pick_at, axis=1) * inside.astype(jnp.float32)
    picked = of_everyone(local_pick, "leaf")
    handed = (picked / leaf_count).astype(jnp.bfloat16)
    received_all = passed_along(handed, "level", 1)
    factor = jnp.where(section_index == 0, root_score, received_all).astype(jnp.float32)
    results = gathered * factor[..., None]
    return results[None]


def solution(mesh):
    in_specs = (
        P("group", None),
        P("level", "leaf", "group", None, None),
        P("level", "leaf", "group", None),
        P("level", "leaf", "group", None),
        P("level", "group", None),
        P("group", None),
        P("group", None),
    )
    out_specs = P("level", "group", None, "leaf")
    return jax.shard_map(body, mesh=mesh, in_specs=in_specs, out_specs=out_specs, check_vma=False)
```

profile of v0, /device:TPU:1, one launch (start us, length us, event | category | flops | bytes accessed | tf_op | source)
XLA Modules:
  0.0 243.8 jit_solution(17947266854259070890)
XLA Ops:
  0.0 0.8 copy.28
  0.9 0.1 reshape_squeeze.3
  1.1 0.9 reduce-window.6
  2.0 0.2 slice_reduce_fusion
  2.2 0.1 mul.111
  2.5 0.5 copy-done.3
  3.0 2.9 %scatter_custom_fusion = s32[768]{0:T(1024)S(1)} fusion(s32[384]{0:T(512)S(1)} %fusion.18, s32[384]{0:T(512)S(1)} %iota.11, s32[]{:T(128)} %constant.128.clone.1), kind=kCustom, calls=%fused_computation.63 | custom fusion | bytes 3076 | tf_op jit(solution)/shard_map/scatter | solution.py:69
  6.0 5.0 %gather_fusion.2 = bf16[768]{0:T(1024)(128)(2,1)S(1)} fusion(bf16[384]{0:T(512)(128)(2,1)S(1)} %reshape.240, s32[1024]{0:T(1024)S(1)} %pad_clamp_fusion.1), kind=kCustom, calls=%fused_computation.2 | custom fusion | bytes 6144 | tf_op jit(solution)/shard_map/jit(_take)/gather | solution.py:76
  11.0 0.7 reshape.304
  11.7 12.0 %all-to-all-start.1 = ((bf16[32,1,24]{2,1,0:T(2,128)(2,1)}), bf16[32,1,24]{2,1,0:T(2,128)(2,1)S(1)}, u32[]{:S(2)}, u32[]{:S(2)}) async-start(bf16[32,1,24]{2,1,0:T(2,128)(2,1)} %reshape.304), calls=%async_computation.1 | async-start | bytes 32768 | tf_op jit(solution)/shard_map/all_to_all | solution.py:95
  23.8 0.7 reshape.244
  24.5 0.6 pad_clamp_fusion.2
  25.1 0.7 broadcast_in_dim.69
  25.8 3.6 %gather_fusion = bf16[768,2048]{1,0:T(8,128)(2,1)S(1)} fusion(bf16[96,2048]{1,0:T(8,128)(2,1)S(1)} %copy-done, s32[1024]{0:T(1024)} %pad_clamp_fusion.2), kind=kCustom, calls=%fused_computation | custom fusion | bytes 6294528 | tf_op jit(solution)/shard_map/jit(_take)/gather | solution.py:73
  29.3 2.7 %select_multiply_fusion = bf16[32,1,24,2048]{3,2,1,0:T(8,128)(2,1)} fusion(bf16[32,1,24,2048]{3,2,1,0:T(8,128)(2,1)S(1)} %bitcast.65, pred[32,24]{1,0:T(8,128)(4,1)} %broadcast_in_dim.69, bf16[32,24]{1,0:T(8,128)(2,1)} %reshape.244), kind=kLoop, calls=%fused_computation.11 | loop fusion | flops 3145728 | bytes 6293760 | tf_op jit(solution)/shard_map/mul | solution.py:73
  32.1 0.3 all-to-all-done.1
  32.4 0.6 copy-done.2
  33.0 8.9 %all-to-all-start = ((bf16[32,1,24,2048]{3,2,1,0:T(8,128)(2,1)}), bf16[32,1,24,2048]{3,2,1,0:T(8,128)(2,1)S(1)}, u32[]{:S(2)}, u32[]{:S(2)}) async-start(bf16[32,1,24,2048]{3,2,1,0:T(8,128)(2,1)} %select_multiply_fusion), calls=%async_computation | async-start | bytes 6291456 | tf_op jit(solution)/shard_map/all_to_all | solution.py:94
  41.9 0.7 and_reduce_fusion
  42.6 0.5 and.56
  43.2 0.7 convert_bitcast_fusion
  43.8 0.7 broadcast_bitcast_fusion
  44.5 0.6 broadcast_clamp_fusion
  45.1 0.7 convert_element_type.57
  45.8 67.3 %all-to-all-done = bf16[32,1,24,2048]{3,2,1,0:T(8,128)(2,1)S(1)} async-done(((bf16[32,1,24,2048]{3,2,1,0:T(8,128)(2,1)}), bf16[32,1,24,2048]{3,2,1,0:T(8,128)(2,1)S(1)}, u32[]{:S(2)}, u32[]{:S(2)}) %all-to-all-start) | async-done | bytes 3145760 | tf_op jit(solution)/shard_map/all_to_all | solution.py:94
  113.1 7.3 %fusion = f32[32,24,1024]{2,1,0:T(8,128)} fusion(bf16[1,1,1,2048,1024]{4,3,2,1,0:T(8,128)(2,1)} %param.8, bf16[32,1,24,2048]{3,2,1,0:T(8,128)(2,1)S(1)} %all-to-all-done, bf16[2048]{0:T(1024)(128)(2,1)} %broadcast_bitcast_fusion), kind=kOutput, calls=%fused_computation.6 | convolution fusion | flops 3222798336 | bytes 10489856 | tf_op jit(solution)/shard_map/cond/branch_1_fun/sjcd,jdl->sjcl/dot_general | solution.py:82
  120.4 8.9 %copy.33 = f32[32,24,1024]{0,1,2:T(8,128)} copy(f32[32,24,1024]{2,1,0:T(8,128)} %fusion) | data formatting | bytes 6291456 | tf_op jit(solution)/shard_map/cond/branch_1_fun/sjcd,jdl->sjcl/dot_general | solution.py:82
  129.3 15.7 %gather_fusion.1 = f32[1024,32,24]{1,2,0:T(8,128)} fusion(f32[32,24,1024]{0,1,2:T(8,128)} %copy.33, s32[1024]{0:T(1024)S(1)} %copy-done.5), kind=kCustom, calls=%fused_computation.1 | custom fusion | bytes 6295552 | tf_op jit(solution)/shard_map/cond/branch_1_fun/jit(take_along_axis)/gather | solution.py:83
  144.9 7.7 %copy.34 = f32[32,1,24,4,256]{4,2,1,0,3:T(8,128)S(1)} copy(f32[32,1,24,4,256]{0,2,4,3,1:T(8,128)} %bitcast.64) | data formatting | bytes 6291456 | tf_op jit(solution)/shard_map/cond/branch_1_fun/jit(take_along_axis)/gather | solution.py:83
  152.7 1.5 multiply_bitcast_fusion
  154.1 36.8 %all_to_all.25 = f32[4,32,1,24,256]{4,3,2,1,0:T(8,128)S(1)} all-to-all(f32[4,32,1,24,256]{4,3,2,1,0:T(8,128)S(1)} %multiply_bitcast_fusion), channel_id=1, replica_groups=mesh['level'=2,'group'=32,'leaf'=4] {'leaf'}, dimensions={0} | all-to-all | bytes 6291456 | tf_op jit(solution)/shard_map/all_to_all | solution.py:16
  190.9 1.1 reduce_sum.36
  192.1 11.6 %all-to-all-start.3 = ((f32[32,1,24,256]{3,2,1,0:T(8,128)}), f32[32,1,24,256]{3,2,1,0:T(8,128)S(1)}, u32[]{:S(2)}, u32[]{:S(2)}) async-start(f32[32,1,24,256]{3,2,1,0:T(8,128)} %bitcast.66), calls=%async_computation.3 | async-start | bytes 1572864 | tf_op jit(solution)/shard_map/all_to_all | solution.py:99
  203.8 0.8 compare_and_fusion
  204.6 0.2 broadcast_in_dim.78
  204.9 0.1 copy.45
  205.0 0.2 mul.123
  205.3 0.1 copy.42
  205.7 16.4 %all-to-all-done.3 = f32[32,1,24,256]{3,2,1,0:T(8,128)S(1)} async-done(((f32[32,1,24,256]{3,2,1,0:T(8,128)}), f32[32,1,24,256]{3,2,1,0:T(8,128)S(1)}, u32[]{:S(2)}, u32[]{:S(2)}) %all-to-all-start.3) | async-done | bytes 786464 | tf_op jit(solution)/shard_map/all_to_all | solution.py:99
  222.1 1.7 gather_fusion.3
  223.7 0.1 gather.35
  223.9 3.5 %gather_fusion.4 = f32[384]{0:T(512)S(1)} fusion(f32[96,1024]{1,0:T(8,128)S(1)} %select_multiply_fusion.1, s32[384]{0:T(512)S(1)} %reshape.280), kind=kCustom, calls=%fused_computation.4 | custom fusion | bytes 6144 | tf_op jit(solution)/shard_map/jit(take_along_axis)/gather | solution.py:110
  227.7 6.5 %all_to_all.26 = f32[4,96,4]{1,2,0:T(4,128)S(1)} all-to-all(f32[4,96,4]{1,2,0:T(4,128)S(1)} %broadcast_in_dim.82), channel_id=1, replica_groups=mesh['level'=2,'group'=32,'leaf'=4] {'leaf'}, dimensions={0} | all-to-all | bytes 12288 | tf_op jit(solution)/shard_map/all_to_all | solution.py:22
  234.2 1.3 collective-permute-start
  235.5 0.1 gather.34
  235.6 7.0 %collective-permute-done = bf16[96,4]{0,1:T(4,128)(2,1)S(1)} collective-permute-done((bf16[96,4]{0,1:T(4,128)(2,1)S(1)}, bf16[96,4]{0,1:T(4,128)(2,1)S(1)}, u32[]{:S(2)}, u32[]{:S(2)}) %collective-permute-start) | collective-permute-done | bytes 800 | tf_op jit(solution)/shard_map/ppermute | solution.py:35
  242.6 0.1 copy.47
  242.7 1.0 select_multiply_fusion.2
  (47 shorter events, 1.2 us)
Async XLA Ops:
  0.0 25.8 %copy-start = (bf16[96,2048]{1,0:T(8,128)(2,1)S(1)}, bf16[96,2048]{1,0:T(8,128)(2,1)}, u32[]{:S(2)}) copy-start(bf16[96,2048]{1,0:T(8,128)(2,1)} %param.7) | copy-start | bytes 1179652
  0.8 5.1 %copy-start.1 = (s32[1,96,4]{2,1,0:T(8,128)}, s32[1,96,4]{2,1,0:T(8,128)S(1)}, u32[]{:S(2)}) copy-start(s32[1,96,4]{2,1,0:T(8,128)S(1)} %copy.28) | copy-start | bytes 4612
  2.4 0.6 copy-start.3
  3.0 2.9 %copy-start.7 = (s32[384]{0:T(512)}, s32[384]{0:T(512)S(1)}, u32[]{:S(2)}) copy-start(s32[384]{0:T(512)S(1)} %fusion.18) | copy-start | bytes 4612
  11.7 20.7 %all-to-all-start.1 = ((bf16[32,1,24]{2,1,0:T(2,128)(2,1)}), bf16[32,1,24]{2,1,0:T(2,128)(2,1)S(1)}, u32[]{:S(2)}, u32[]{:S(2)}) async-start(bf16[32,1,24]{2,1,0:T(2,128)(2,1)} %reshape.304), calls=%async_computation.1 | async-start | bytes 32768 | tf_op jit(solution)/shard_map/all_to_all | solution.py:95
  32.4 0.6 copy-start.2
  33.0 80.1 %all-to-all-start = ((bf16[32,1,24,2048]{3,2,1,0:T(8,128)(2,1)}), bf16[32,1,24,2048]{3,2,1,0:T(8,128)(2,1)S(1)}, u32[]{:S(2)}, u32[]{:S(2)}) async-start(bf16[32,1,24,2048]{3,2,1,0:T(8,128)(2,1)} %select_multiply_fusion), calls=%async_computation | async-start | bytes 6291456 | tf_op jit(solution)/shard_map/all_to_all | solution.py:94
  120.4 8.9 %copy-start.5 = (s32[1024]{0:T(1024)S(1)}, s32[1024]{0:T(1024)}, u32[]{:S(2)}) copy-start(s32[1024]{0:T(1024)} %broadcast_clamp_fusion) | copy-start | bytes 12292
  190.9 12.7 %copy-start.4 = (s32[384]{0:T(512)S(1)}, s32[384]{0:T(512)}, u32[]{:S(2)}) copy-start(s32[384]{0:T(512)} %copy-done.3) | copy-start | bytes 4612
  190.9 13.9 %copy-start.9 = (bf16[96,4]{0,1:T(4,128)(2,1)S(1)}, bf16[96,4]{0,1:T(4,128)(2,1)}, u32[]{:S(2)}) copy-start(bf16[96,4]{0,1:T(4,128)(2,1)} %param.12) | copy-start | bytes 2308
  190.9 14.3 %copy-start.6 = (s32[96,4]{0,1:T(4,128)S(1)}, s32[96,4]{0,1:T(4,128)}, u32[]{:S(2)}) copy-start(s32[96,4]{0,1:T(4,128)} %param.13) | copy-start | bytes 4612
  190.9 14.7 %copy-start.8 = (s32[384]{0:T(512)S(1)}, s32[384]{0:T(512)}, u32[]{:S(2)}) copy-start(s32[384]{0:T(512)} %copy-done.7) | copy-start | bytes 4612
  192.1 30.0 %all-to-all-start.3 = ((f32[32,1,24,256]{3,2,1,0:T(8,128)}), f32[32,1,24,256]{3,2,1,0:T(8,128)S(1)}, u32[]{:S(2)}, u32[]{:S(2)}) async-start(f32[32,1,24,256]{3,2,1,0:T(8,128)} %bitcast.66), calls=%async_computation.3 | async-start | bytes 1572864 | tf_op jit(solution)/shard_map/all_to_all | solution.py:99
  234.2 8.4 %collective-permute-start = (bf16[96,4]{0,1:T(4,128)(2,1)S(1)}, bf16[96,4]{0,1:T(4,128)(2,1)S(1)}, u32[]{:S(2)}, u32[]{:S(2)}) collective-permute-start(bf16[96,4]{0,1:T(4,128)(2,1)S(1)} %multiply_convert_fusion), channel_id=1, source_target_pairs={{0,128},{1,129},{2,130},{3,131},{4,132},{5,133},{6,134},{7,135},{8... | collective-permute-start | bytes 2312 | tf_op jit(solution)/shard_map/ppermute | solution.py:35
where the time goes:
time: 245 us; the launch traced here: 244 us
  waiting for transfers between devices  91 us (37%)
  local copies, waits for them, and re-layouts  56.2 us (23%)
  blocking collectives  43.3 us (18%)
  starting transfers between devices  33.8 us (14%)
  other arithmetic  11.9 us (5%)
  matrix products  7.28 us (3%)
    all_to_all x1, waiting for transfers between devices, body(): lax.all_to_all(routed, 'group', split_axis=0, concat_axis=0, tiled=True)  67.3 us
    all_to_all x1, blocking collectives, sent_and_summed(): lax.all_to_all(cut_along(value, dim, peers), axis, 0, 0, tiled=True)  36.8 us
    gather x2, local copies, waits for them, and re-layouts, compute(): logits = jnp.take_along_axis(logits, column_map[None, :, None, :], axis=3)  23.4 us
    all_to_all x1, waiting for transfers between devices, body(): lax.all_to_all(summed, 'group', split_axis=0, concat_axis=0, tiled=True)  16.4 us
    all_to_all x1, starting transfers between devices, body(): lax.all_to_all(routed_parent, 'group', split_axis=0, concat_axis=0, tiled...  12 us
    all_to_all x1, starting transfers between devices, body(): lax.all_to_all(summed, 'group', split_axis=0, concat_axis=0, tiled=True)  11.6 us
    all_to_all x1, starting transfers between devices, body(): lax.all_to_all(routed, 'group', split_axis=0, concat_axis=0, tiled=True)  8.91 us
    dot_general x1, local copies, waits for them, and re-layouts, compute(): jnp.einsum('sjcd,jdl->sjcl', kept_rows, scorer, preferred_element_type=jn...  8.88 us
  transfers between devices with their start and end apart: 4, of which 4 were waited for; matrix products, arithmetic and copies ran while one was open for 6% of the time, Pallas kernels for 0%

commit v1 on v0

v1 whole, which is shorter than its diff:
```python
import functools

import jax
import jax.numpy as jnp
from jax import lax
from jax.experimental import pallas as pl
from jax.experimental.pallas import tpu as pltpu
from jax.sharding import PartitionSpec as P

QBLK = 32
CAP = 8
ROWS_OF_CHIPS = 4
MESH = pl.DeviceIdType.MESH
F32, BF16, I32 = jnp.float32, jnp.bfloat16, jnp.int32


def exact_parts(value):
    high = value.astype(BF16)
    rest = value - high.astype(F32)
    middle = rest.astype(BF16)
    return high, middle, (rest - middle.astype(F32)).astype(BF16)


def wait_for(ref, sem):
    pltpu.make_async_copy(ref, ref, sem).wait()


def kernel(
    groups,
    leaves,
    cap,
    q_ref,
    w_ref,
    mask_ref,
    map_ref,
    beam_ref,
    root_ref,
    pos_ref,
    out_ref,
    w_in,
    w_own,
    perm,
    picked,
    rows_in,
    scored,
    half_left,
    half_right,
    block_left,
    block_right,
    total,
    returned,
    choose,
    columns,
    line,
    parent_out,
    parent_in,
    w_sem,
    yz_send,
    yz_recv,
    fwd_send,
    fwd_recv,
    rel_send,
    rel_recv,
    half_send,
    half_recv,
    block_send,
    block_recv,
    ret_send,
    ret_recv,
    parent_send,
    parent_recv,
):
    level = lax.axis_index("level")
    g = lax.axis_index("group")
    x = lax.axis_index("leaf")
    ny = ROWS_OF_CHIPS
    nz = groups // ny
    y, z = g // nz, g % nz
    right, left, across = (x + 1) % leaves, (x + leaves - 1) % leaves, (x + 2) % leaves
    beam_len, queries = beam_ref.shape
    feature, labels = w_ref.shape
    part = feature // leaves
    share = labels // leaves
    slots = groups * cap
    chunk = nz * cap
    half = chunk // 2

    weight_copy = pltpu.make_async_copy(w_ref, w_in, w_sem)
    weight_copy.start()

    barrier = pltpu.get_barrier_semaphore()

    def greet(o, carry):
        pl.semaphore_signal(
            barrier, inc=1, device_id={"group": (g + o) % groups}, device_id_type=MESH
        )
        return carry

    lax.fori_loop(1, groups, greet, 0)
    for other in (left, right):
        pl.semaphore_signal(barrier, inc=1, device_id={"leaf": other}, device_id_type=MESH)
    for other in range(leaves):
        pl.semaphore_signal(
            barrier,
            inc=1,
            device_id={"level": 1 - level, "leaf": other},
            device_id_type=MESH,
        )

    beam = beam_ref[...]
    group_id = lax.broadcasted_iota(I32, (groups, queries), 0)
    hit = jnp.zeros((groups, queries), F32)
    for b in range(beam_len):
        hit = hit + (beam[b : b + 1, :] == group_id).astype(F32)
    earlier = (
        lax.broadcasted_iota(I32, (queries, queries), 0)
        < lax.broadcasted_iota(I32, (queries, queries), 1)
    ).astype(F32)
    rank = jnp.dot(hit.astype(BF16), earlier.astype(BF16), preferred_element_type=F32)
    place = group_id.astype(F32) * cap + rank
    slot = [
        jnp.sum(jnp.where(beam[b : b + 1, :] == group_id, place, 0.0), axis=0, keepdims=True)
        for b in range(beam_len)
    ]
    slot_id = lax.broadcasted_iota(I32, (slots, queries), 0).astype(F32)
    select = jnp.zeros((slots, queries), F32)
    for b in range(beam_len):
        select = select + (slot[b] == slot_id).astype(F32)
    own_part = q_ref[:, pl.ds(pl.multiple_of(x * part, 128), part)]
    chosen_rows = jnp.dot(select.astype(BF16), own_part, preferred_element_type=F32)
    picked[...] = chosen_rows.astype(BF16).reshape(slots // 8, 8, part)

    pl.semaphore_wait(barrier, groups - 1 + 2 + leaves)

    def slot_rows(group):
        return pl.ds(pl.multiple_of(group * cap, 8), cap)

    def slot_blocks(group):
        return pl.ds(group * (cap // 8), cap // 8)

    def chunk_blocks(step):
        return pl.ds(((y + step) % ny) * (chunk // 8), chunk // 8)

    def chunk_half(step, which):
        return pl.ds(((y + step) % ny) * (chunk // 8) + which * (half // 8), half // 8)

    pltpu.make_async_copy(
        picked.at[slot_blocks(g)], rows_in.at[x, slot_blocks(g)], yz_recv.at[0]
    ).start()

    def send_rows(n, carry):
        step = n // nz
        to = ((y + ny - step) % ny) * nz + (z + n) % nz
        pltpu.make_async_remote_copy(
            src_ref=picked.at[slot_blocks(to)],
            dst_ref=rows_in.at[x, slot_blocks(g)],
            send_sem=yz_send,
            recv_sem=yz_recv.at[step],
            device_id={"group": to},
            device_id_type=MESH,
        ).start()
        return carry

    lax.fori_loop(1, groups, send_rows, 0)

    tile = 256
    mask_rows = feature // mask_ref.shape[0]

    def fill_perm(n, carry):
        at = pl.ds(pl.multiple_of(n * tile, tile), tile)
        column = lax.broadcasted_iota(I32, (tile, labels), 0) + n * tile
        perm[at, :] = (column == map_ref[...]).astype(F32).astype(BF16)
        return carry

    lax.fori_loop(0, labels // tile, fill_perm, 0)
    weight_copy.wait()

    def permute(n, carry):
        row = n // (labels // tile)
        at = pl.ds(pl.multiple_of((n % (labels // tile)) * tile, tile), tile)
        product = jnp.dot(
            w_in[pl.ds(pl.multiple_of(row * tile, tile), tile), :],
            perm[:, at],
            preferred_element_type=F32,
        )
        for m in range(tile // mask_rows):
            keep = mask_ref[row * (tile // mask_rows) + m].astype(F32)
            w_own[pl.ds(pl.multiple_of(row * tile + m * mask_rows, mask_rows), mask_rows), at] = (
                product[m * mask_rows : (m + 1) * mask_rows] * keep
            ).astype(BF16)
        return carry

    lax.fori_loop(0, (feature // tile) * (labels // tile), permute, 0)

    pos = pos_ref[...]
    parent_slot, parent_label = pos // labels, (pos % labels).astype(F32)
    root = root_ref[...].astype(F32)
    line[...] = jnp.zeros_like(line)
    for b in range(beam_len):
        line[b : b + 1, :queries] = slot[b]
        line[2 * beam_len + b : 2 * beam_len + b + 1, :queries] = parent_label[b : b + 1]
        line[3 * beam_len + b : 3 * beam_len + b + 1, :queries] = root[b : b + 1]
        slot_of = jnp.zeros((1, queries), F32)
        root_of = jnp.zeros((1, queries), F32)
        for s in range(beam_len):
            same = parent_slot[b : b + 1] == s
            slot_of = slot_of + jnp.where(same, slot[s], 0.0)
            root_of = root_of + jnp.where(same, root[s : s + 1], 0.0)
        line[beam_len + b : beam_len + b + 1, :queries] = slot_of
        line[4 * beam_len + b : 4 * beam_len + b + 1, :queries] = root_of
    columns[...] = jnp.transpose(line[...])
    across_slots = lax.broadcasted_iota(I32, (queries, slots), 1).astype(F32)
    for b in range(2 * beam_len):
        choose[b * queries : (b + 1) * queries, :] = (
            (columns[:queries, b : b + 1] == across_slots).astype(F32).astype(BF16)
        )

    def to_leaf(src, dst, send, recv, other):
        pltpu.make_async_remote_copy(
            src_ref=src,
            dst_ref=dst,
            send_sem=send,
            recv_sem=recv,
            device_id={"leaf": other},
            device_id_type=MESH,
        ).start()

    def stage(t, carry):
        @pl.when(t < ny)
        def _():
            own = rows_in.at[x, chunk_blocks(t)]
            wait_for(own, yz_recv.at[t])
            to_leaf(own, own, fwd_send, fwd_recv.at[0, t], right)
            to_leaf(own, own, fwd_send, fwd_recv.at[1, t], left)

        @pl.when((t >= 1) & (t < ny + 1))
        def _():
            c = t - 1
            wait_for(rows_in.at[left, chunk_blocks(c)], fwd_recv.at[0, c])
            first = rows_in.at[left, chunk_half(c, 0)]
            to_leaf(first, first, rel_send, rel_recv.at[0, c], right)
            wait_for(rows_in.at[right, chunk_blocks(c)], fwd_recv.at[1, c])
            second = rows_in.at[right, chunk_half(c, 1)]
            to_leaf(second, second, rel_send, rel_recv.at[1, c], left)

        @pl.when((t >= 2) & (t < ny + 2))
        def _():
            c = t - 2
            wait_for(rows_in.at[across, chunk_half(c, 0)], rel_recv.at[0, c])
            wait_for(rows_in.at[across, chunk_half(c, 1)], rel_recv.at[1, c])

            def score(n, carry):
                j = (across + n) % leaves
                at = pl.ds(pl.multiple_of(j * share, 128), share)
                logits = jnp.zeros((chunk, share), F32)
                for p in range(leaves):
                    logits = logits + jnp.dot(
                        rows_in[p, chunk_blocks(c)].reshape(chunk, part),
                        w_own[p * part : (p + 1) * part, at],
                        preferred_element_type=F32,
                    )
                scored[c, j] = jax.nn.sigmoid(logits)
                return carry

            lax.fori_loop(0, leaves, score, 0)
            to_leaf(
                scored.at[c, across, pl.ds(0, half)],
                half_left.at[c],
                half_send,
                half_recv.at[0, c],
                right,
            )
            to_leaf(
                scored.at[c, across, pl.ds(half, half)],
                half_right.at[c],
                half_send,
                half_recv.at[1, c],
                left,
            )

        @pl.when((t >= 3) & (t < ny + 3))
        def _():
            c = t - 3
            wait_for(half_left.at[c], half_recv.at[0, c])
            scored[c, right, :half] = scored[c, right, :half] + half_left[c]
            to_leaf(
                scored.at[c, right], block_left.at[c], block_send, block_recv.at[0, c], right
            )
            wait_for(half_right.at[c], half_recv.at[1, c])
            scored[c, left, half:] = scored[c, left, half:] + half_right[c]
            to_leaf(
                scored.at[c, left], block_right.at[c], block_send, block_recv.at[1, c], left
            )

        @pl.when(t >= 4)
        def _():
            c = t - 4
            wait_for(block_left.at[c], block_recv.at[0, c])
            wait_for(block_right.at[c], block_recv.at[1, c])
            total[c] = scored[c, x] + (block_left[c] + block_right[c])
            row = ((y + c) % ny) * nz

            def send_back(n, carry):
                zz = (z + n) % nz
                pltpu.make_async_remote_copy(
                    src_ref=total.at[c, slot_rows(zz)],
                    dst_ref=returned.at[slot_rows(g)],
                    send_sem=ret_send,
                    recv_sem=ret_recv,
                    device_id={"group": row + zz},
                    device_id_type=MESH,
                ).start()
                return carry

            @pl.when(c == 0)
            def _():
                pltpu.make_async_copy(
                    total.at[c, slot_rows(z)], returned.at[slot_rows(g)], ret_recv
                ).start()

            @pl.when(c > 0)
            def _():
                send_back(0, 0)

            lax.fori_loop(1, nz, send_back, 0)

        return carry

    lax.fori_loop(0, ny + 4, stage, 0)

    wait_for(returned, ret_recv)
    high, middle, low = exact_parts(returned[...])
    entries = beam_len * queries

    def gather(at):
        chosen = choose[at, :]
        return (
            jnp.dot(chosen, high, preferred_element_type=F32)
            + jnp.dot(chosen, middle, preferred_element_type=F32)
        ) + jnp.dot(chosen, low, preferred_element_type=F32)

    def to_level_one(other, carry):
        pltpu.make_async_remote_copy(
            src_ref=parent_out,
            dst_ref=parent_in.at[x],
            send_sem=parent_send,
            recv_sem=parent_recv,
            device_id={"level": 1, "leaf": other},
            device_id_type=MESH,
        ).start()
        return carry

    @pl.when(level == 0)
    def _():
        lane = lax.broadcasted_iota(I32, (queries, share), 1).astype(F32) + (x * share).astype(F32)
        wide = lax.broadcasted_iota(I32, (queries, 128), 1)
        sums = gather(slice(entries, 2 * entries))
        parents = jnp.zeros((queries, 128), F32)
        for b in range(beam_len):
            at_label = columns[:queries, 2 * beam_len + b : 2 * beam_len + b + 1] == lane
            mine = jnp.where(at_label, sums[b * queries : (b + 1) * queries], 0.0)
            value = jnp.sum(mine, axis=1, keepdims=True) * columns[
                :queries, 4 * beam_len + b : 4 * beam_len + b + 1
            ]
            parents = jnp.where(wide == b, value, parents)
        parent_out[...] = parents
        lax.fori_loop(0, leaves, to_level_one, 0)

    sums = gather(slice(0, entries))

    @pl.when(level == 0)
    def _():
        for b in range(beam_len):
            out_ref[b] = (
                sums[b * queries : (b + 1) * queries]
                * columns[:queries, 3 * beam_len + b : 3 * beam_len + b + 1]
            )

        wait_for(parent_in, parent_send)

    @pl.when(level == 1)
    def _():
        wait_for(parent_in, parent_recv)
        parents = parent_in[0]
        for n in range(1, leaves):
            parents = parents + parent_in[n]
        parents = (parents / leaves).astype(BF16).astype(F32)
        for b in range(beam_len):
            out_ref[b] = sums[b * queries : (b + 1) * queries] * parents[:, b : b + 1]

    wait_for(picked.at[pl.ds(0, (groups - 1) * cap // 8)], yz_send)
    wait_for(rows_in.at[pl.ds(0, 2)], fwd_send)
    wait_for(rows_in.at[0], rel_send)
    wait_for(total, half_send)
    wait_for(scored.at[:, pl.ds(0, 2)], block_send)
    wait_for(returned.at[pl.ds(0, (groups - 1) * cap)], ret_send)


def body(queries, weights, block_mask, label_map, beam_lists, root_score, parent_pos):
    groups, leaves = lax.axis_size("group"), lax.axis_size("leaf")
    rows, feature = queries.shape
    labels = weights.shape[4]
    beam_len = beam_lists.shape[2]
    cap = rows // QBLK * CAP
    slots = groups * cap
    ny = ROWS_OF_CHIPS
    chunk = slots // ny
    half = chunk // 2
    share = labels // leaves
    vmem = pl.BlockSpec(memory_space=pltpu.VMEM)
    dma = pltpu.SemaphoreType.DMA
    out = pl.pallas_call(
        functools.partial(kernel, groups, leaves, cap),
        out_shape=jax.ShapeDtypeStruct((beam_len, rows, share), F32),
        in_specs=[
            vmem,
            pl.BlockSpec(memory_space=pl.ANY),
            pl.BlockSpec(memory_space=pltpu.SMEM),
            vmem,
            vmem,
            vmem,
            vmem,
        ],
        out_specs=vmem,
        scratch_shapes=[
            pltpu.VMEM((feature, labels), BF16),
            pltpu.VMEM((feature, labels), BF16),
            pltpu.VMEM((labels, labels), BF16),
            pltpu.VMEM((slots // 8, 8, feature // leaves), BF16),
            pltpu.VMEM((leaves, slots // 8, 8, feature // leaves), BF16),
            pltpu.VMEM((ny, leaves, chunk, share), F32),
            pltpu.VMEM((ny, half, share), F32),
            pltpu.VMEM((ny, half, share), F32),
            pltpu.VMEM((ny, chunk, share), F32),
            pltpu.VMEM((ny, chunk, share), F32),
            pltpu.VMEM((ny, chunk, share), F32),
            pltpu.VMEM((slots, share), F32),
            pltpu.VMEM((2 * beam_len * rows, slots), BF16),
            pltpu.VMEM((128, 128), F32),
            pltpu.VMEM((128, 128), F32),
            pltpu.VMEM((rows, 128), F32),
            pltpu.VMEM((leaves, rows, 128), F32),
            dma,
            dma,
            dma((ny,)),
            dma,
            dma((2, ny)),
            dma,
            dma((2, ny)),
            dma,
            dma((2, ny)),
            dma,
            dma((2, ny)),
            dma,
            dma,
            dma,
            dma,
        ],
        compiler_params=pltpu.CompilerParams(
            collective_id=0, has_side_effects=True, vmem_limit_bytes=48 << 20
        ),
    )(
        queries,
        weights[0, 0, 0],
        block_mask[0, 0, 0],
        label_map[0, 0],
        beam_lists[0].T,
        root_score.T,
        parent_pos.T,
    )
    return jnp.transpose(out, (1, 0, 2))[None]


def solution(mesh):
    in_specs = (
        P("group", None),
        P("level", "leaf", "group", None, None),
        P("level", "leaf", "group", None),
        P("level", "leaf", "group", None),
        P("level", "group", None),
        P("group", None),
        P("group", None),
    )
    out_specs = P("level", "group", None, "leaf")
    return jax.shard_map(body, mesh=mesh, in_specs=in_specs, out_specs=out_specs, check_vma=False)
```

time: 245 us -> 96.5 us (0.39)
  waiting for transfers between devices: 91 us -> 0 us
  Pallas kernels: 0 us -> 88.6 us
  local copies, waits for them, and re-layouts: 56.2 us -> 7.57 us
  blocking collectives: 43.3 us -> 0 us
  starting transfers between devices: 33.8 us -> 0 us
  other arithmetic: 11.9 us -> 0 us
  matrix products: 7.28 us -> 0 us
    pallas_call x0 -> x1, Pallas kernels: none -> 88.6 us  [body(): pl.pallas_call(functools.partial(kernel, groups, leaves, cap), out_shape=...]
    all_to_all x3 -> x0, waiting for transfers between devices: 84 us -> none  [the longest x1 67.3 us: body(): lax.all_to_all(routed, 'group', split_axis=0, concat_axis=0, tiled=True)]
    all_to_all x2 -> x0, blocking collectives: 43.3 us -> none  [the longest x1 36.8 us: sent_and_summed(): lax.all_to_all(cut_along(value, dim, peers), axis, 0, 0, tiled=True)]
    gather x10 -> x0, local copies, waits for them, and re-layouts: 37.5 us -> none  [the longest x2 23.4 us: compute(): logits = jnp.take_along_axis(logits, column_map[None, :, None, :], axis=3)]
    all_to_all x3 -> x0, starting transfers between devices: 32.5 us -> none  [the longest x1 12 us: body(): lax.all_to_all(routed_parent, 'group', split_axis=0, concat_axis=0, tiled...]
    dot_general x1 -> x0, local copies, waits for them, and re-layouts: 8.88 us -> none  [compute(): jnp.einsum('sjcd,jdl->sjcl', kept_rows, scorer, preferred_element_type=jn...]
    dot_general x1 -> x0, matrix products: 7.28 us -> none  [compute(): jnp.einsum('sjcd,jdl->sjcl', kept_rows, scorer, preferred_element_type=jn...]
    ppermute x1 -> x0, waiting for transfers between devices: 6.99 us -> none  [passed_along(): return lax.ppermute(block, axis, route)]
  transfers between devices with their start and end apart: 4 -> 0, of which waited for: 4 -> 0; matrix products, arithmetic and copies ran while one was open for 6% -> 0% of each run, Pallas kernels for 0% -> 0%
where the time goes in v1:
time: 96.5 us; the launch traced here: 96.2 us
  Pallas kernels  88.6 us (92%)
  local copies, waits for them, and re-layouts  7.57 us (8%)
    pallas_call x1, Pallas kernels, body(): pl.pallas_call(functools.partial(kernel, groups, leaves, cap), out_shape=...  88.6 us
    unnamed x14, local copies, waits for them, and re-layouts  6.56 us

profile of v1, /device:TPU:1, one launch (start us, length us, event | category | flops | bytes accessed | tf_op | source)
XLA Modules:
  0.0 96.2 jit_solution(17199544989060764239)
XLA Ops:
  0.0 0.0 copy-start
  0.0 2.2 %copy-done = bf16[1,1,1,2048,1024]{4,3,2,1,0:T(8,128)(2,1)S(1)} copy-done((bf16[1,1,1,2048,1024]{4,3,2,1,0:T(8,128)(2,1)S(1)}, bf16[1,1,1,2048,1024]{4,3,2,1,0:T(8,128)(2,1)}, u32[]{:S(2)}) %copy-start) | copy-done | bytes 4194328
  2.2 0.0 copy-start.1
  2.2 1.0 %copy-done.1 = bf16[96,2048]{1,0:T(8,128)(2,1)S(1)} copy-done((bf16[96,2048]{1,0:T(8,128)(2,1)S(1)}, bf16[96,2048]{1,0:T(8,128)(2,1)}, u32[]{:S(2)}) %copy-start.1) | copy-done | bytes 393240
  3.2 0.0 copy-start.2
  3.2 0.7 copy-done.2
  3.9 0.0 copy-start.3
  3.9 0.7 copy-done.3
  4.6 0.0 copy-start.4
  4.6 0.7 copy-done.4
  5.2 0.0 copy-start.5
  5.2 0.7 copy-done.5
  5.9 0.0 copy-start.6
  5.9 0.7 copy-done.6
  6.6 88.6 %shard_map.73 = f32[4,96,256]{2,1,0:T(8,128)S(1)} custom-call(bf16[96,2048]{1,0:T(8,128)(2,1)S(1)} %copy-done.1, bf16[2048,1024]{1,0:T(8,128)(2,1)S(1)} %bitcast.11, s32[16]{0:T(128)S(1)} %bitcast.17, s32[1,1024]{1,0:T(1,128)S(1)} %bitcast.13, s32[4,96]{1,0:T(4,128)S(1)} %bitcast.14, bf16[4,96]{1,0:T(4,128)(2,1)S(1)} %bitcast.16, s32[4,96]{1,0:T(4,128)S(1)} %bitcast.15), custom_call_target="tpu_custom_call" | custom-call | tf_op jit(solution)/shard_map/pallas_call | solution.py:412
  95.2 1.0 %copy.8 = f32[1,96,4,256]{3,2,1,0:T(4,128)} copy(f32[1,96,4,256]{3,1,2,0:T(8,128)S(1)} %bitcast.12) | data formatting | bytes 786432 | tf_op jit(solution)/shard_map/broadcast_in_dim | solution.py:471
Async XLA Ops:
  0.0 2.2 %copy-start = (bf16[1,1,1,2048,1024]{4,3,2,1,0:T(8,128)(2,1)S(1)}, bf16[1,1,1,2048,1024]{4,3,2,1,0:T(8,128)(2,1)}, u32[]{:S(2)}) copy-start(bf16[1,1,1,2048,1024]{4,3,2,1,0:T(8,128)(2,1)} %param.8) | copy-start | bytes 12582916
  2.2 1.0 %copy-start.1 = (bf16[96,2048]{1,0:T(8,128)(2,1)S(1)}, bf16[96,2048]{1,0:T(8,128)(2,1)}, u32[]{:S(2)}) copy-start(bf16[96,2048]{1,0:T(8,128)(2,1)} %q_ref.1) | copy-start | bytes 1179652
  3.2 0.7 copy-start.2
  3.9 0.7 copy-start.3
  4.6 0.7 copy-start.4
  5.2 0.7 copy-start.5
  5.9 0.7 copy-start.6

commit v2 on v1

--- a/solution.py
+++ b/solution.py
@@ -11,14 +11,21 @@
 CAP = 8
 ROWS_OF_CHIPS = 4
 MESH = pl.DeviceIdType.MESH
-F32, BF16, I32 = jnp.float32, jnp.bfloat16, jnp.int32
-
-
-def exact_parts(value):
+F32, BF16, I32, I16 = jnp.float32, jnp.bfloat16, jnp.int32, jnp.int16
+
+
+def encode(value):
+    octaves = jnp.log2(jnp.maximum(value, 2.0**-61))
+    return jnp.round((octaves + 29.0) * 1024.0).astype(I32).astype(I16)
+
+
+def decode(code):
+    return jnp.exp2(code.astype(I32).astype(F32) * (1.0 / 1024.0) - 29.0)
+
+
+def two_parts(value):
     high = value.astype(BF16)
-    rest = value - high.astype(F32)
-    middle = rest.astype(BF16)
-    return high, middle, (rest - middle.astype(F32)).astype(BF16)
+    return high, (value - high.astype(F32)).astype(BF16)
 
 
 def wait_for(ref, sem):
@@ -29,20 +36,28 @@
     groups,
     leaves,
     cap,
+    q_hbm,
+    w_ref,
+    mask_hbm,
+    map_hbm,
+    beam_hbm,
+    root_hbm,
+    pos_hbm,
+    out_ref,
     q_ref,
-    w_ref,
     mask_ref,
     map_ref,
     beam_ref,
     root_ref,
     pos_ref,
-    out_ref,
     w_in,
     w_own,
     perm,
     picked,
     rows_in,
     scored,
+    half_out,
+    block_out,
     half_left,
     half_right,
     block_left,
@@ -54,6 +69,7 @@
     line,
     parent_out,
     parent_in,
+    in_sem,
     w_sem,
     yz_send,
     yz_recv,
@@ -85,6 +101,21 @@
     chunk = nz * cap
     half = chunk // 2
 
+    copies = [
+        pltpu.make_async_copy(src, dst, in_sem.at[n])
+        for n, (src, dst) in enumerate(
+            (
+                (beam_hbm, beam_ref),
+                (q_hbm, q_ref),
+                (map_hbm, map_ref),
+                (mask_hbm, mask_ref),
+                (pos_hbm, pos_ref),
+                (root_hbm, root_ref),
+            )
+        )
+    ]
+    for copy in copies:
+        copy.start()
     weight_copy = pltpu.make_async_copy(w_ref, w_in, w_sem)
     weight_copy.start()
 
@@ -107,6 +138,8 @@
             device_id_type=MESH,
         )
 
+    for copy in copies[:2]:
+        copy.wait()
     beam = beam_ref[...]
     group_id = lax.broadcasted_iota(I32, (groups, queries), 0)
     hit = jnp.zeros((groups, queries), F32)
@@ -132,9 +165,6 @@
 
     pl.semaphore_wait(barrier, groups - 1 + 2 + leaves)
 
-    def slot_rows(group):
-        return pl.ds(pl.multiple_of(group * cap, 8), cap)
-
     def slot_blocks(group):
         return pl.ds(group * (cap // 8), cap // 8)
 
@@ -163,6 +193,8 @@
 
     lax.fori_loop(1, groups, send_rows, 0)
 
+    for copy in copies[2:]:
+        copy.wait()
     tile = 256
     mask_rows = feature // mask_ref.shape[0]
 
@@ -263,15 +295,16 @@
                 return carry
 
             lax.fori_loop(0, leaves, score, 0)
+            half_out[c] = encode(scored[c, across])
             to_leaf(
-                scored.at[c, across, pl.ds(0, half)],
+                half_out.at[c, pl.ds(0, half)],
                 half_left.at[c],
                 half_send,
                 half_recv.at[0, c],
                 right,
             )
             to_leaf(
-                scored.at[c, across, pl.ds(half, half)],
+                half_out.at[c, pl.ds(half, half)],
                 half_right.at[c],
                 half_send,
                 half_recv.at[1, c],
@@ -282,14 +315,16 @@
         def _():
             c = t - 3
             wait_for(half_left.at[c], half_recv.at[0, c])
-            scored[c, right, :half] = scored[c, right, :half] + half_left[c]
+            block_out[c, 0, :half] = encode(scored[c, right, :half] + decode(half_left[c]))
+            block_out[c, 0, half:] = encode(scored[c, right, half:])
             to_leaf(
-                scored.at[c, right], block_left.at[c], block_send, block_recv.at[0, c], right
+                block_out.at[c, 0], block_left.at[c], block_send, block_recv.at[0, c], right
             )
             wait_for(half_right.at[c], half_recv.at[1, c])
-            scored[c, left, half:] = scored[c, left, half:] + half_right[c]
+            block_out[c, 1, :half] = encode(scored[c, left, :half])
+            block_out[c, 1, half:] = encode(scored[c, left, half:] + decode(half_right[c]))
             to_leaf(
-                scored.at[c, left], block_right.at[c], block_send, block_recv.at[1, c], left
+                block_out.at[c, 1], block_right.at[c], block_send, block_recv.at[1, c], left
             )
 
         @pl.when(t >= 4)
@@ -297,14 +332,15 @@
             c = t - 4
             wait_for(block_left.at[c], block_recv.at[0, c])
             wait_for(block_right.at[c], block_recv.at[1, c])
-            total[c] = scored[c, x] + (block_left[c] + block_right[c])
+            sums = scored[c, x] + (decode(block_left[c]) + decode(block_right[c]))
+            total[c] = encode(sums.reshape(chunk // 8, 8, share))
             row = ((y + c) % ny) * nz
 
             def send_back(n, carry):
                 zz = (z + n) % nz
                 pltpu.make_async_remote_copy(
-                    src_ref=total.at[c, slot_rows(zz)],
-                    dst_ref=returned.at[slot_rows(g)],
+                    src_ref=total.at[c, slot_blocks(zz)],
+                    dst_ref=returned.at[slot_blocks(g)],
                     send_sem=ret_send,
                     recv_sem=ret_recv,
                     device_id={"group": row + zz},
@@ -315,7 +351,7 @@
             @pl.when(c == 0)
             def _():
                 pltpu.make_async_copy(
-                    total.at[c, slot_rows(z)], returned.at[slot_rows(g)], ret_recv
+                    total.at[c, slot_blocks(z)], returned.at[slot_blocks(g)], ret_recv
                 ).start()
 
             @pl.when(c > 0)
@@ -329,15 +365,14 @@
     lax.fori_loop(0, ny + 4, stage, 0)
 
     wait_for(returned, ret_recv)
-    high, middle, low = exact_parts(returned[...])
+    high, low = two_parts(decode(returned[...]).reshape(slots, share))
     entries = beam_len * queries
 
     def gather(at):
         chosen = choose[at, :]
-        return (
-            jnp.dot(chosen, high, preferred_element_type=F32)
-            + jnp.dot(chosen, middle, preferred_element_type=F32)
-        ) + jnp.dot(chosen, low, preferred_element_type=F32)
+        return jnp.dot(chosen, high, preferred_element_type=F32) + jnp.dot(
+            chosen, low, preferred_element_type=F32
+        )
 
     def to_level_one(other, carry):
         pltpu.make_async_remote_copy(
@@ -391,9 +426,9 @@
     wait_for(picked.at[pl.ds(0, (groups - 1) * cap // 8)], yz_send)
     wait_for(rows_in.at[pl.ds(0, 2)], fwd_send)
     wait_for(rows_in.at[0], rel_send)
-    wait_for(total, half_send)
-    wait_for(scored.at[:, pl.ds(0, 2)], block_send)
-    wait_for(returned.at[pl.ds(0, (groups - 1) * cap)], ret_send)
+    wait_for(half_out, half_send)
+    wait_for(block_out, block_send)
+    wait_for(returned.at[pl.ds(0, (groups - 1) * cap // 8)], ret_send)
 
 
 def body(queries, weights, block_mask, label_map, beam_lists, root_score, parent_pos):
@@ -412,34 +447,35 @@
     out = pl.pallas_call(
         functools.partial(kernel, groups, leaves, cap),
         out_shape=jax.ShapeDtypeStruct((beam_len, rows, share), F32),
-        in_specs=[
-            vmem,
-            pl.BlockSpec(memory_space=pl.ANY),
-            pl.BlockSpec(memory_space=pltpu.SMEM),
-            vmem,
-            vmem,
-            vmem,
-            vmem,
-        ],
+        in_specs=[pl.BlockSpec(memory_space=pltpu.HBM)] * 7,
         out_specs=vmem,
         scratch_shapes=[
+            pltpu.VMEM((rows, feature), BF16),
+            pltpu.SMEM((block_mask.shape[3],), I32),
+            pltpu.VMEM((1, labels), I32),
+            pltpu.VMEM((beam_len, rows), I32),
+            pltpu.VMEM((beam_len, rows), BF16),
+            pltpu.VMEM((beam_len, rows), I32),
             pltpu.VMEM((feature, labels), BF16),
             pltpu.VMEM((feature, labels), BF16),
             pltpu.VMEM((labels, labels), BF16),
             pltpu.VMEM((slots // 8, 8, feature // leaves), BF16),
             pltpu.VMEM((leaves, slots // 8, 8, feature // leaves), BF16),
             pltpu.VMEM((ny, leaves, chunk, share), F32),
-            pltpu.VMEM((ny, half, share), F32),
-            pltpu.VMEM((ny, half, share), F32),
-            pltpu.VMEM((ny, chunk, share), F32),
-            pltpu.VMEM((ny, chunk, share), F32),
-            pltpu.VMEM((ny, chunk, share), F32),
-            pltpu.VMEM((slots, share), F32),
+            pltpu.VMEM((ny, chunk, share), I16),
+            pltpu.VMEM((ny, 2, chunk, share), I16),
+            pltpu.VMEM((ny, half, share), I16),
+            pltpu.VMEM((ny, half, share), I16),
+            pltpu.VMEM((ny, chunk, share), I16),
+            pltpu.VMEM((ny, chunk, share), I16),
+            pltpu.VMEM((ny, chunk // 8, 8, share), I16),
+            pltpu.VMEM((slots // 8, 8, share), I16),
             pltpu.VMEM((2 * beam_len * rows, slots), BF16),
             pltpu.VMEM((128, 128), F32),
             pltpu.VMEM((128, 128), F32),
             pltpu.VMEM((rows, 128), F32),
             pltpu.VMEM((leaves, rows, 128), F32),
+            dma((6,)),
             dma,
             dma,
             dma((ny,)),
@@ -457,7 +493,7 @@
             dma,
         ],
         compiler_params=pltpu.CompilerParams(
-            collective_id=0, has_side_effects=True, vmem_limit_bytes=48 << 20
+            collective_id=0, has_side_effects=True, vmem_limit_bytes=60 << 20
         ),
     )(
         queries,

time: 96.5 us -> 78.8 us (0.82)
  Pallas kernels: 88.6 us -> 76.7 us
  local copies, waits for them, and re-layouts: 7.57 us -> 2 us
    pallas_call x1, Pallas kernels: 88.6 us -> 76.7 us  [body(): pl.pallas_call(functools.partial(kernel, groups, leaves, cap), out_shape=...]
    unnamed x14 -> x0, local copies, waits for them, and re-layouts: 6.56 us -> none
    broadcast_in_dim x1, local copies, waits for them, and re-layouts: 1 us -> 2 us  [body(): return jnp.transpose(out, (1, 0, 2))[None]]
where the time goes in v2:
time: 78.8 us; the launch traced here: 78.7 us
  Pallas kernels  76.7 us (97%)
  local copies, waits for them, and re-layouts  2 us (3%)
    pallas_call x1, Pallas kernels, body(): pl.pallas_call(functools.partial(kernel, groups, leaves, cap), out_shape=...  76.7 us
    broadcast_in_dim x1, local copies, waits for them, and re-layouts, body(): return jnp.transpose(out, (1, 0, 2))[None]  2 us

profile of v2, /device:TPU:1, one launch (start us, length us, event | category | flops | bytes accessed | tf_op | source)
XLA Modules:
  0.0 78.7 jit_solution(2824671567048307226)
XLA Ops:
  0.0 76.7 %shard_map.73 = f32[4,96,256]{2,1,0:T(8,128)} custom-call(bf16[96,2048]{1,0:T(8,128)(2,1)} %q_hbm.1, bf16[2048,1024]{1,0:T(8,128)(2,1)} %bitcast.11, s32[16]{0:T(128)} %bitcast.17, s32[1,1024]{1,0:T(1,128)} %bitcast.13, s32[4,96]{1,0:T(4,128)} %bitcast.14, bf16[4,96]{1,0:T(4,128)(2,1)} %bitcast.16, s32[4,96]{1,0:T(4,128)} %bitcast.15), custom_call_target="tpu_custom_call" | custom-call | tf_op jit(solution)/shard_map/pallas_call | solution.py:447
  76.7 2.0 %copy.8 = f32[1,96,4,256]{3,2,1,0:T(4,128)} copy(f32[1,96,4,256]{3,1,2,0:T(8,128)} %bitcast.12) | data formatting | bytes 786432 | tf_op jit(solution)/shard_map/broadcast_in_dim | solution.py:507

commit v3 on v2

--- a/solution.py
+++ b/solution.py
@@ -53,6 +53,11 @@
     w_in,
     w_own,
     perm,
+    spread,
+    beams_own,
+    beams_in,
+    hits,
+    select,
     picked,
     rows_in,
     scored,
@@ -71,12 +76,14 @@
     parent_in,
     in_sem,
     w_sem,
-    yz_send,
-    yz_recv,
+    beam_send,
+    beam_recv,
+    z_send,
+    z_recv,
+    y_send,
+    y_recv,
     fwd_send,
     fwd_recv,
-    rel_send,
-    rel_recv,
     half_send,
     half_recv,
     block_send,
@@ -93,6 +100,9 @@
     nz = groups // ny
     y, z = g // nz, g % nz
     right, left, across = (x + 1) % leaves, (x + leaves - 1) % leaves, (x + 2) % leaves
+    fetched = 2 * (x % 2)
+    other_two = 2 - fetched
+    own_part = fetched + level
     beam_len, queries = beam_ref.shape
     feature, labels = w_ref.shape
     part = feature // leaves
@@ -130,11 +140,25 @@
     lax.fori_loop(1, groups, greet, 0)
     for other in (left, right):
         pl.semaphore_signal(barrier, inc=1, device_id={"leaf": other}, device_id_type=MESH)
-    for other in range(leaves):
+    for n in range(1, leaves):
         pl.semaphore_signal(
             barrier,
             inc=1,
-            device_id={"level": 1 - level, "leaf": other},
+            device_id={"level": 1 - level, "leaf": (x + n) % leaves},
+            device_id_type=MESH,
+        )
+    for n in range(nz):
+        pl.semaphore_signal(
+            barrier,
+            inc=1,
+            device_id={"level": 1 - level, "group": y * nz + (z + n) % nz},
+            device_id_type=MESH,
+        )
+    for n in range(1, ny):
+        pl.semaphore_signal(
+            barrier,
+            inc=1,
+            device_id={"level": 1 - level, "group": ((y + n) % ny) * nz + z},
             device_id_type=MESH,
         )
 
@@ -155,43 +179,130 @@
         jnp.sum(jnp.where(beam[b : b + 1, :] == group_id, place, 0.0), axis=0, keepdims=True)
         for b in range(beam_len)
     ]
-    slot_id = lax.broadcasted_iota(I32, (slots, queries), 0).astype(F32)
-    select = jnp.zeros((slots, queries), F32)
-    for b in range(beam_len):
-        select = select + (slot[b] == slot_id).astype(F32)
-    own_part = q_ref[:, pl.ds(pl.multiple_of(x * part, 128), part)]
-    chosen_rows = jnp.dot(select.astype(BF16), own_part, preferred_element_type=F32)
-    picked[...] = chosen_rows.astype(BF16).reshape(slots // 8, 8, part)
-
-    pl.semaphore_wait(barrier, groups - 1 + 2 + leaves)
-
-    def slot_blocks(group):
-        return pl.ds(group * (cap // 8), cap // 8)
-
-    def chunk_blocks(step):
-        return pl.ds(((y + step) % ny) * (chunk // 8), chunk // 8)
-
-    def chunk_half(step, which):
-        return pl.ds(((y + step) % ny) * (chunk // 8) + which * (half // 8), half // 8)
-
-    pltpu.make_async_copy(
-        picked.at[slot_blocks(g)], rows_in.at[x, slot_blocks(g)], yz_recv.at[0]
-    ).start()
-
-    def send_rows(n, carry):
-        step = n // nz
-        to = ((y + ny - step) % ny) * nz + (z + n) % nz
+    spread[0] = q_ref[:, pl.ds(pl.multiple_of(own_part * part, 128), part)]
+    beams_own[...] = jnp.full_like(beams_own, -1)
+    beams_own[:beam_len, :queries] = beam
+
+    pl.semaphore_wait(barrier, groups - 1 + 2 + leaves - 1 + nz + ny - 1)
+
+    def along_z(src, dst, at, step):
         pltpu.make_async_remote_copy(
-            src_ref=picked.at[slot_blocks(to)],
-            dst_ref=rows_in.at[x, slot_blocks(g)],
-            send_sem=yz_send,
-            recv_sem=yz_recv.at[step],
-            device_id={"group": to},
+            src_ref=src,
+            dst_ref=dst,
+            send_sem=z_send,
+            recv_sem=z_recv.at[at],
+            device_id={"group": y * nz + (z + nz + step) % nz},
             device_id_type=MESH,
         ).start()
+
+    pltpu.make_async_copy(beams_own, beams_in.at[level * nz], beam_recv).start()
+    for n in range(nz):
+        at = 2 * n if n < nz // 2 else 2 * (nz - n) - 1
+        for flip in range(2):
+            if n or flip:
+                pltpu.make_async_remote_copy(
+                    src_ref=beams_own,
+                    dst_ref=beams_in.at[level * nz + at],
+                    send_sem=beam_send,
+                    recv_sem=beam_recv,
+                    device_id={
+                        "level": (level + flip) % 2,
+                        "group": y * nz + (z + n) % nz,
+                    },
+                    device_id_type=MESH,
+                ).start()
+    along_z(spread.at[0], spread.at[2], 2, 1)
+    along_z(spread.at[0], spread.at[1], 1, -1)
+
+    wait_for(beams_in, beam_recv)
+    eight = lax.broadcasted_iota(I32, (8, 128), 0)
+    near_group = jnp.where(eight < ny, eight * nz + z, -2)
+
+    def find_hits(n, carry):
+        names = beams_in[n]
+        found = jnp.zeros((8, 128), F32)
+        for b in range(beam_len):
+            found = found + (names[b : b + 1, :] == near_group).astype(F32)
+        hits[pl.ds(pl.multiple_of(n * 8, 8), 8), :] = found
         return carry
 
-    lax.fori_loop(1, groups, send_rows, 0)
+    lax.fori_loop(0, 2 * nz, find_hits, 0)
+    before = (
+        lax.broadcasted_iota(I32, (128, 128), 0) < lax.broadcasted_iota(I32, (128, 128), 1)
+    ).astype(F32)
+    hits[...] = jnp.dot(
+        hits[...].astype(BF16), before.astype(BF16), preferred_element_type=F32
+    )
+    near_slot = lax.broadcasted_iota(I32, (ny * cap, 128), 0).astype(F32)
+
+    def make_select(n, carry):
+        names = beams_in[n]
+        place = eight.astype(F32) * cap + hits[pl.ds(pl.multiple_of(n * 8, 8), 8), :] + 1.0
+        chosen = jnp.zeros((ny * cap, 128), F32)
+        for b in range(beam_len):
+            at = jnp.sum(
+                jnp.where(names[b : b + 1, :] == near_group, place, 0.0), axis=0, keepdims=True
+            )
+            chosen = chosen + (at - 1.0 == near_slot).astype(F32)
+        select[n % nz, pl.ds(pl.multiple_of((n // nz) * ny * cap, 16), ny * cap), :] = chosen.astype(
+            BF16
+        )
+        return carry
+
+    lax.fori_loop(0, 2 * nz, make_select, 0)
+
+    blocks = cap // 8
+
+    def slot_blocks(group):
+        return pl.ds(group * blocks, blocks)
+
+    def chunk_blocks(step):
+        return pl.ds(step * (chunk // 8), chunk // 8)
+
+    def distance_blocks(at):
+        return pl.ds(at * (half // 8), half // 8)
+
+    def pick(at):
+        rows = jnp.dot(select[at, :, :queries], spread[at], preferred_element_type=F32)
+        picked[pl.ds(at * (chunk // 8), chunk // 8)] = rows.astype(BF16).reshape(
+            chunk // 8, 8, part
+        )
+
+        def send_rows(n, carry):
+            to_level, to_row = (level + n // ny) % 2, (y + n) % ny
+            pltpu.make_async_remote_copy(
+                src_ref=picked.at[slot_blocks((at * 2 + to_level) * ny + to_row)],
+                dst_ref=rows_in.at[own_part, slot_blocks(at * ny + y)],
+                send_sem=y_send,
+                recv_sem=y_recv.at[at // 2],
+                device_id={"level": to_level, "group": to_row * nz + z},
+                device_id_type=MESH,
+            ).start()
+            return carry
+
+        pltpu.make_async_copy(
+            picked.at[slot_blocks((at * 2 + level) * ny + y)],
+            rows_in.at[own_part, slot_blocks(at * ny + y)],
+            y_recv.at[at // 2],
+        ).start()
+        lax.fori_loop(1, 2 * ny, send_rows, 0)
+
+    def to_leaf(src, dst, send, recv, other):
+        pltpu.make_async_remote_copy(
+            src_ref=src,
+            dst_ref=dst,
+            send_sem=send,
+            recv_sem=recv,
+            device_id={"leaf": other},
+            device_id_type=MESH,
+        ).start()
+
+    def exchange(c):
+        two = pl.ds(fetched, 2)
+        wait_for(rows_in.at[two, chunk_blocks(c)], y_recv.at[c])
+        for n, other in enumerate((right, left)):
+            rows = rows_in.at[two, distance_blocks(2 * c + n)]
+            to_leaf(rows, rows, fwd_send, fwd_recv.at[n, c], other)
 
     for copy in copies[2:]:
         copy.wait()
@@ -222,7 +333,30 @@
             ).astype(BF16)
         return carry
 
-    lax.fori_loop(0, (feature // tile) * (labels // tile), permute, 0)
+    tiles = (feature // tile) * (labels // tile)
+    for c in range(ny):
+        up, down = 2 * c, 2 * c + 1
+        if c:
+            wait_for(spread.at[up], z_recv.at[up])
+            if c < ny - 1:
+                along_z(spread.at[up], spread.at[up + 2], up + 2, 1)
+            else:
+                top = pl.ds(0, queries // 2)
+                along_z(spread.at[up, top], spread.at[nz - 1, top], nz - 1, 1)
+        else:
+            pick(0)
+        wait_for(spread.at[down], z_recv.at[down])
+        if c < ny - 2:
+            along_z(spread.at[down], spread.at[down + 2], down + 2, -1)
+        elif c == ny - 2:
+            low = pl.ds(queries // 2, queries // 2)
+            along_z(spread.at[down, low], spread.at[nz - 1, low], nz - 1, -1)
+        if c:
+            pick(up)
+        pick(down)
+        if c >= 2:
+            exchange(c - 2)
+        lax.fori_loop(tiles * c // ny, tiles * (c + 1) // ny, permute, 0)
 
     pos = pos_ref[...]
     parent_slot, parent_label = pos // labels, (pos % labels).astype(F32)
@@ -247,39 +381,17 @@
             (columns[:queries, b : b + 1] == across_slots).astype(F32).astype(BF16)
         )
 
-    def to_leaf(src, dst, send, recv, other):
-        pltpu.make_async_remote_copy(
-            src_ref=src,
-            dst_ref=dst,
-            send_sem=send,
-            recv_sem=recv,
-            device_id={"leaf": other},
-            device_id_type=MESH,
-        ).start()
-
     def stage(t, carry):
+        @pl.when(t < 2)
+        def _():
+            exchange(t + ny - 2)
+
         @pl.when(t < ny)
         def _():
-            own = rows_in.at[x, chunk_blocks(t)]
-            wait_for(own, yz_recv.at[t])
-            to_leaf(own, own, fwd_send, fwd_recv.at[0, t], right)
-            to_leaf(own, own, fwd_send, fwd_recv.at[1, t], left)
-
-        @pl.when((t >= 1) & (t < ny + 1))
-        def _():
-            c = t - 1
-            wait_for(rows_in.at[left, chunk_blocks(c)], fwd_recv.at[0, c])
-            first = rows_in.at[left, chunk_half(c, 0)]
-            to_leaf(first, first, rel_send, rel_recv.at[0, c], right)
-            wait_for(rows_in.at[right, chunk_blocks(c)], fwd_recv.at[1, c])
-            second = rows_in.at[right, chunk_half(c, 1)]
-            to_leaf(second, second, rel_send, rel_recv.at[1, c], left)
-
-        @pl.when((t >= 2) & (t < ny + 2))
-        def _():
-            c = t - 2
-            wait_for(rows_in.at[across, chunk_half(c, 0)], rel_recv.at[0, c])
-            wait_for(rows_in.at[across, chunk_half(c, 1)], rel_recv.at[1, c])
+            c = t
+            two = pl.ds(other_two, 2)
+            for n in range(2):
+                wait_for(rows_in.at[two, distance_blocks(2 * c + n)], fwd_recv.at[n, c])
 
             def score(n, carry):
                 j = (across + n) % leaves
@@ -311,9 +423,9 @@
                 left,
             )
 
-        @pl.when((t >= 3) & (t < ny + 3))
+        @pl.when((t >= 1) & (t < ny + 1))
         def _():
-            c = t - 3
+            c = t - 1
             wait_for(half_left.at[c], half_recv.at[0, c])
             block_out[c, 0, :half] = encode(scored[c, right, :half] + decode(half_left[c]))
             block_out[c, 0, half:] = encode(scored[c, right, half:])
@@ -327,23 +439,23 @@
                 block_out.at[c, 1], block_right.at[c], block_send, block_recv.at[1, c], left
             )
 
-        @pl.when(t >= 4)
+        @pl.when(t >= 2)
         def _():
-            c = t - 4
+            c = t - 2
             wait_for(block_left.at[c], block_recv.at[0, c])
             wait_for(block_right.at[c], block_recv.at[1, c])
             sums = scored[c, x] + (decode(block_left[c]) + decode(block_right[c]))
             total[c] = encode(sums.reshape(chunk // 8, 8, share))
-            row = ((y + c) % ny) * nz
 
             def send_back(n, carry):
-                zz = (z + n) % nz
+                row = (y + n) % ny
+                place = jnp.where(n < ny, z + nz - c, z + c + 1) % nz
                 pltpu.make_async_remote_copy(
-                    src_ref=total.at[c, slot_blocks(zz)],
+                    src_ref=total.at[c, slot_blocks((n // ny) * ny + row)],
                     dst_ref=returned.at[slot_blocks(g)],
                     send_sem=ret_send,
                     recv_sem=ret_recv,
-                    device_id={"group": row + zz},
+                    device_id={"group": row * nz + place},
                     device_id_type=MESH,
                 ).start()
                 return carry
@@ -351,18 +463,18 @@
             @pl.when(c == 0)
             def _():
                 pltpu.make_async_copy(
-                    total.at[c, slot_blocks(z)], returned.at[slot_blocks(g)], ret_recv
+                    total.at[c, slot_blocks(y)], returned.at[slot_blocks(g)], ret_recv
                 ).start()
 
             @pl.when(c > 0)
             def _():
                 send_back(0, 0)
 
-            lax.fori_loop(1, nz, send_back, 0)
+            lax.fori_loop(1, 2 * ny, send_back, 0)
 
         return carry
 
-    lax.fori_loop(0, ny + 4, stage, 0)
+    lax.fori_loop(0, ny + 2, stage, 0)
 
     wait_for(returned, ret_recv)
     high, low = two_parts(decode(returned[...]).reshape(slots, share))
@@ -423,9 +535,10 @@
         for b in range(beam_len):
             out_ref[b] = sums[b * queries : (b + 1) * queries] * parents[:, b : b + 1]
 
-    wait_for(picked.at[pl.ds(0, (groups - 1) * cap // 8)], yz_send)
+    wait_for(beams_in.at[pl.ds(0, 2 * nz - 1)], beam_send)
+    wait_for(spread.at[pl.ds(0, nz - 1)], z_send)
+    wait_for(picked.at[pl.ds(0, (2 * groups - nz) * blocks)], y_send)
     wait_for(rows_in.at[pl.ds(0, 2)], fwd_send)
-    wait_for(rows_in.at[0], rel_send)
     wait_for(half_out, half_send)
     wait_for(block_out, block_send)
     wait_for(returned.at[pl.ds(0, (groups - 1) * cap // 8)], ret_send)
@@ -439,6 +552,7 @@
     cap = rows // QBLK * CAP
     slots = groups * cap
     ny = ROWS_OF_CHIPS
+    nz = groups // ny
     chunk = slots // ny
     half = chunk // 2
     share = labels // leaves
@@ -459,7 +573,12 @@
             pltpu.VMEM((feature, labels), BF16),
             pltpu.VMEM((feature, labels), BF16),
             pltpu.VMEM((labels, labels), BF16),
-            pltpu.VMEM((slots // 8, 8, feature // leaves), BF16),
+            pltpu.VMEM((nz, rows, feature // leaves), BF16),
+            pltpu.VMEM((8, 128), I32),
+            pltpu.VMEM((2 * nz, 8, 128), I32),
+            pltpu.VMEM((16 * nz, 128), F32),
+            pltpu.VMEM((nz, chunk, 128), BF16),
+            pltpu.VMEM((2 * slots // 8, 8, feature // leaves), BF16),
             pltpu.VMEM((leaves, slots // 8, 8, feature // leaves), BF16),
             pltpu.VMEM((ny, leaves, chunk, share), F32),
             pltpu.VMEM((ny, chunk, share), I16),
@@ -478,9 +597,11 @@
             dma((6,)),
             dma,
             dma,
+            dma,
+            dma,
+            dma((nz,)),
+            dma,
             dma((ny,)),
-            dma,
-            dma((2, ny)),
             dma,
             dma((2, ny)),
             dma,

time: 78.8 us -> 79.1 us (level)
  no operation moved by 1% of the time
where the time goes in v3:
time: 79.1 us; the launch traced here: 78.9 us
  Pallas kernels  76.9 us (97%)
  local copies, waits for them, and re-layouts  2 us (3%)
    pallas_call x1, Pallas kernels, body(): pl.pallas_call(functools.partial(kernel, groups, leaves, cap), out_shape=...  76.9 us
    broadcast_in_dim x1, local copies, waits for them, and re-layouts, body(): return jnp.transpose(out, (1, 0, 2))[None]  2 us

profile of v3, /device:TPU:1, one launch (start us, length us, event | category | flops | bytes accessed | tf_op | source)
XLA Modules:
  0.0 78.9 jit_solution(8720830607864814215)
XLA Ops:
  0.0 76.9 %shard_map.73 = f32[4,96,256]{2,1,0:T(8,128)} custom-call(bf16[96,2048]{1,0:T(8,128)(2,1)} %q_hbm.1, bf16[2048,1024]{1,0:T(8,128)(2,1)} %bitcast.11, s32[16]{0:T(128)} %bitcast.17, s32[1,1024]{1,0:T(1,128)} %bitcast.13, s32[4,96]{1,0:T(4,128)} %bitcast.14, bf16[4,96]{1,0:T(4,128)(2,1)} %bitcast.16, s32[4,96]{1,0:T(4,128)} %bitcast.15), custom_call_target="tpu_custom_call" | custom-call | tf_op jit(solution)/shard_map/pallas_call | solution.py:561
  76.9 2.0 %copy.8 = f32[1,96,4,256]{3,2,1,0:T(4,128)} copy(f32[1,96,4,256]{3,1,2,0:T(8,128)} %bitcast.12) | data formatting | bytes 786432 | tf_op jit(solution)/shard_map/broadcast_in_dim | solution.py:628

commit v4 on v3

--- a/solution.py
+++ b/solution.py
@@ -59,6 +59,7 @@
     hits,
     select,
     picked,
+    passing,
     rows_in,
     scored,
     half_out,
@@ -82,6 +83,9 @@
     z_recv,
     y_send,
     y_recv,
+    via_send,
+    via_recv,
+    pass_send,
     fwd_send,
     fwd_recv,
     half_send,
@@ -185,12 +189,15 @@
 
     pl.semaphore_wait(barrier, groups - 1 + 2 + leaves - 1 + nz + ny - 1)
 
-    def along_z(src, dst, at, step):
+    def half_rows(which):
+        return pl.ds(which * (queries // 2), queries // 2)
+
+    def along_z(come, at, which, step):
         pltpu.make_async_remote_copy(
-            src_ref=src,
-            dst_ref=dst,
+            src_ref=spread.at[come, half_rows(which)],
+            dst_ref=spread.at[at, half_rows(which)],
             send_sem=z_send,
-            recv_sem=z_recv.at[at],
+            recv_sem=z_recv.at[at, which],
             device_id={"group": y * nz + (z + nz + step) % nz},
             device_id_type=MESH,
         ).start()
@@ -211,8 +218,9 @@
                     },
                     device_id_type=MESH,
                 ).start()
-    along_z(spread.at[0], spread.at[2], 2, 1)
-    along_z(spread.at[0], spread.at[1], 1, -1)
+    for which in range(2):
+        along_z(0, 2, which, 1)
+        along_z(0, 1, which, -1)
 
     wait_for(beams_in, beam_recv)
     eight = lax.broadcasted_iota(I32, (8, 128), 0)
@@ -264,28 +272,34 @@
 
     def pick(at):
         rows = jnp.dot(select[at, :, :queries], spread[at], preferred_element_type=F32)
-        picked[pl.ds(at * (chunk // 8), chunk // 8)] = rows.astype(BF16).reshape(
-            chunk // 8, 8, part
-        )
-
-        def send_rows(n, carry):
-            to_level, to_row = (level + n // ny) % 2, (y + n) % ny
+        picked[at] = rows.astype(BF16).reshape(2, ny, blocks, 8, part)
+        pltpu.make_async_copy(
+            picked.at[at, level, y], rows_in.at[own_part, slot_blocks(at * ny + y)], y_recv.at[at // 2]
+        ).start()
+        for flip, step in ((0, 2), (1, 2), (0, 1), (0, 3), (1, 1), (1, 3), (1, 0)):
+            to_level, to_row = (level + flip) % 2, (y + step) % ny
             pltpu.make_async_remote_copy(
-                src_ref=picked.at[slot_blocks((at * 2 + to_level) * ny + to_row)],
+                src_ref=picked.at[at, to_level, to_row],
                 dst_ref=rows_in.at[own_part, slot_blocks(at * ny + y)],
                 send_sem=y_send,
                 recv_sem=y_recv.at[at // 2],
                 device_id={"level": to_level, "group": to_row * nz + z},
                 device_id_type=MESH,
             ).start()
-            return carry
-
-        pltpu.make_async_copy(
-            picked.at[slot_blocks((at * 2 + level) * ny + y)],
-            rows_in.at[own_part, slot_blocks(at * ny + y)],
-            y_recv.at[at // 2],
-        ).start()
-        lax.fori_loop(1, 2 * ny, send_rows, 0)
+
+    def pass_on(at):
+        came_from = (y + (ny - 1 if at % 2 == 0 else 1)) % ny
+        wait_for(passing.at[at], via_recv.at[at])
+        for flip in range(2):
+            to_level = (level + flip) % 2
+            pltpu.make_async_remote_copy(
+                src_ref=passing.at[at, to_level],
+                dst_ref=rows_in.at[own_part, slot_blocks(at * ny + came_from)],
+                send_sem=pass_send,
+                recv_sem=y_recv.at[at // 2],
+                device_id={"level": to_level, "group": ((came_from + 2) % ny) * nz + z},
+                device_id_type=MESH,
+            ).start()
 
     def to_leaf(src, dst, send, recv, other):
         pltpu.make_async_remote_copy(
@@ -306,7 +320,7 @@
 
     for copy in copies[2:]:
         copy.wait()
-    tile = 256
+    tile, tall = 256, 1024
     mask_rows = feature // mask_ref.shape[0]
 
     def fill_perm(n, carry):
@@ -322,41 +336,38 @@
         row = n // (labels // tile)
         at = pl.ds(pl.multiple_of((n % (labels // tile)) * tile, tile), tile)
         product = jnp.dot(
-            w_in[pl.ds(pl.multiple_of(row * tile, tile), tile), :],
+            w_in[pl.ds(pl.multiple_of(row * tall, tall), tall), :],
             perm[:, at],
             preferred_element_type=F32,
         )
-        for m in range(tile // mask_rows):
-            keep = mask_ref[row * (tile // mask_rows) + m].astype(F32)
-            w_own[pl.ds(pl.multiple_of(row * tile + m * mask_rows, mask_rows), mask_rows), at] = (
+        for m in range(tall // mask_rows):
+            keep = mask_ref[row * (tall // mask_rows) + m].astype(F32)
+            w_own[pl.ds(pl.multiple_of(row * tall + m * mask_rows, mask_rows), mask_rows), at] = (
                 product[m * mask_rows : (m + 1) * mask_rows] * keep
             ).astype(BF16)
         return carry
 
-    tiles = (feature // tile) * (labels // tile)
-    for c in range(ny):
-        up, down = 2 * c, 2 * c + 1
-        if c:
-            wait_for(spread.at[up], z_recv.at[up])
-            if c < ny - 1:
-                along_z(spread.at[up], spread.at[up + 2], up + 2, 1)
-            else:
-                top = pl.ds(0, queries // 2)
-                along_z(spread.at[up, top], spread.at[nz - 1, top], nz - 1, 1)
-        else:
-            pick(0)
-        wait_for(spread.at[down], z_recv.at[down])
-        if c < ny - 2:
-            along_z(spread.at[down], spread.at[down + 2], down + 2, -1)
-        elif c == ny - 2:
-            low = pl.ds(queries // 2, queries // 2)
-            along_z(spread.at[down, low], spread.at[nz - 1, low], nz - 1, -1)
-        if c:
-            pick(up)
+    tiles = (feature // tall) * (labels // tile)
+    pick(0)
+    for hop in range(1, ny):
+        up, down = 2 * hop, 2 * hop - 1
+        for which in range(2):
+            wait_for(spread.at[up, half_rows(which)], z_recv.at[up, which])
+            if hop < ny - 1 or which == 0:
+                along_z(up, min(up + 2, nz - 1), which, 1)
+            wait_for(spread.at[down, half_rows(which)], z_recv.at[down, which])
+            if hop < ny - 1 or which == 1:
+                along_z(down, down + 2, which, -1)
         pick(down)
-        if c >= 2:
-            exchange(c - 2)
-        lax.fori_loop(tiles * c // ny, tiles * (c + 1) // ny, permute, 0)
+        pick(up)
+        lax.fori_loop(tiles * (hop - 1) // ny, tiles * hop // ny, permute, 0)
+        if hop == ny - 1:
+            exchange(0)
+    for which in range(2):
+        wait_for(spread.at[nz - 1, half_rows(which)], z_recv.at[nz - 1, which])
+    pick(nz - 1)
+    exchange(1)
+    lax.fori_loop(tiles * (ny - 1) // ny, tiles, permute, 0)
 
     pos = pos_ref[...]
     parent_slot, parent_label = pos // labels, (pos % labels).astype(F32)
@@ -393,20 +404,16 @@
             for n in range(2):
                 wait_for(rows_in.at[two, distance_blocks(2 * c + n)], fwd_recv.at[n, c])
 
-            def score(n, carry):
-                j = (across + n) % leaves
-                at = pl.ds(pl.multiple_of(j * share, 128), share)
-                logits = jnp.zeros((chunk, share), F32)
-                for p in range(leaves):
-                    logits = logits + jnp.dot(
-                        rows_in[p, chunk_blocks(c)].reshape(chunk, part),
-                        w_own[p * part : (p + 1) * part, at],
-                        preferred_element_type=F32,
-                    )
-                scored[c, j] = jax.nn.sigmoid(logits)
-                return carry
-
-            lax.fori_loop(0, leaves, score, 0)
+            logits = jnp.zeros((chunk, labels), F32)
+            for p in range(leaves):
+                logits = logits + jnp.dot(
+                    rows_in[p, chunk_blocks(c)].reshape(chunk, part),
+                    w_own[p * part : (p + 1) * part, :],
+                    preferred_element_type=F32,
+                )
+            one_tree = jax.nn.sigmoid(logits)
+            for j in range(leaves):
+                scored[c, j] = one_tree[:, j * share : (j + 1) * share]
             half_out[c] = encode(scored[c, across])
             to_leaf(
                 half_out.at[c, pl.ds(0, half)],
@@ -537,7 +544,7 @@
 
     wait_for(beams_in.at[pl.ds(0, 2 * nz - 1)], beam_send)
     wait_for(spread.at[pl.ds(0, nz - 1)], z_send)
-    wait_for(picked.at[pl.ds(0, (2 * groups - nz) * blocks)], y_send)
+    wait_for(picked.at[pl.ds(0, 7)], y_send)
     wait_for(rows_in.at[pl.ds(0, 2)], fwd_send)
     wait_for(half_out, half_send)
     wait_for(block_out, block_send)
@@ -578,7 +585,8 @@
             pltpu.VMEM((2 * nz, 8, 128), I32),
             pltpu.VMEM((16 * nz, 128), F32),
             pltpu.VMEM((nz, chunk, 128), BF16),
-            pltpu.VMEM((2 * slots // 8, 8, feature // leaves), BF16),
+            pltpu.VMEM((nz, 2, ny, cap // 8, 8, feature // leaves), BF16),
+            pltpu.VMEM((nz, 2, cap // 8, 8, feature // leaves), BF16),
             pltpu.VMEM((leaves, slots // 8, 8, feature // leaves), BF16),
             pltpu.VMEM((ny, leaves, chunk, share), F32),
             pltpu.VMEM((ny, chunk, share), I16),
@@ -599,9 +607,12 @@
             dma,
             dma,
             dma,
+            dma((nz, 2)),
+            dma,
+            dma((ny,)),
+            dma,
             dma((nz,)),
             dma,
-            dma((ny,)),
             dma,
             dma((2, ny)),
             dma,

time: 79.1 us -> 76.1 us (0.962)
  Pallas kernels: 76.9 us -> 74 us
    pallas_call x1, Pallas kernels: 76.9 us -> 74 us  [body(): pl.pallas_call(functools.partial(kernel, groups, leaves, cap), out_shape=...]
where the time goes in v4:
time: 76.1 us; the launch traced here: 76 us
  Pallas kernels  74 us (97%)
  local copies, waits for them, and re-layouts  2 us (3%)
    pallas_call x1, Pallas kernels, body(): pl.pallas_call(functools.partial(kernel, groups, leaves, cap), out_shape=...  74 us
    broadcast_in_dim x1, local copies, waits for them, and re-layouts, body(): return jnp.transpose(out, (1, 0, 2))[None]  2 us

profile of v4, /device:TPU:1, one launch (start us, length us, event | category | flops | bytes accessed | tf_op | source)
XLA Modules:
  0.0 76.0 jit_solution(6196128855901916396)
XLA Ops:
  0.0 74.0 %shard_map.73 = f32[4,96,256]{2,1,0:T(8,128)} custom-call(bf16[96,2048]{1,0:T(8,128)(2,1)} %q_hbm.1, bf16[2048,1024]{1,0:T(8,128)(2,1)} %bitcast.11, s32[16]{0:T(128)} %bitcast.17, s32[1,1024]{1,0:T(1,128)} %bitcast.13, s32[4,96]{1,0:T(4,128)} %bitcast.14, bf16[4,96]{1,0:T(4,128)(2,1)} %bitcast.16, s32[4,96]{1,0:T(4,128)} %bitcast.15), custom_call_target="tpu_custom_call" | custom-call | tf_op jit(solution)/shard_map/pallas_call | solution.py:568
  74.0 2.0 %copy.8 = f32[1,96,4,256]{3,2,1,0:T(4,128)} copy(f32[1,96,4,256]{3,1,2,0:T(8,128)} %bitcast.12) | data formatting | bytes 786432 | tf_op jit(solution)/shard_map/broadcast_in_dim | solution.py:639

commit v5 on v4

--- a/solution.py
+++ b/solution.py
@@ -59,7 +59,6 @@
     hits,
     select,
     picked,
-    passing,
     rows_in,
     scored,
     half_out,
@@ -83,9 +82,6 @@
     z_recv,
     y_send,
     y_recv,
-    via_send,
-    via_recv,
-    pass_send,
     fwd_send,
     fwd_recv,
     half_send,
@@ -192,15 +188,19 @@
     def half_rows(which):
         return pl.ds(which * (queries // 2), queries // 2)
 
-    def along_z(come, at, which, step):
+    def along_z(come, at, step, which=None):
+        rows = pl.ds(0, queries) if which is None else half_rows(which)
         pltpu.make_async_remote_copy(
-            src_ref=spread.at[come, half_rows(which)],
-            dst_ref=spread.at[at, half_rows(which)],
+            src_ref=spread.at[come, rows],
+            dst_ref=spread.at[at, rows],
             send_sem=z_send,
-            recv_sem=z_recv.at[at, which],
+            recv_sem=z_recv.at[at],
             device_id={"group": y * nz + (z + nz + step) % nz},
             device_id_type=MESH,
         ).start()
+
+    def from_z(at):
+        wait_for(spread.at[at], z_recv.at[at])
 
     pltpu.make_async_copy(beams_own, beams_in.at[level * nz], beam_recv).start()
     for n in range(nz):
@@ -218,9 +218,10 @@
                     },
                     device_id_type=MESH,
                 ).start()
-    for which in range(2):
-        along_z(0, 2, which, 1)
-        along_z(0, 1, which, -1)
+    along_z(0, 2, 1)
+    along_z(0, 1, -1)
+    along_z(0, 4, 2)
+    along_z(0, 3, -2)
 
     wait_for(beams_in, beam_recv)
     eight = lax.broadcasted_iota(I32, (8, 128), 0)
@@ -287,20 +288,6 @@
                 device_id_type=MESH,
             ).start()
 
-    def pass_on(at):
-        came_from = (y + (ny - 1 if at % 2 == 0 else 1)) % ny
-        wait_for(passing.at[at], via_recv.at[at])
-        for flip in range(2):
-            to_level = (level + flip) % 2
-            pltpu.make_async_remote_copy(
-                src_ref=passing.at[at, to_level],
-                dst_ref=rows_in.at[own_part, slot_blocks(at * ny + came_from)],
-                send_sem=pass_send,
-                recv_sem=y_recv.at[at // 2],
-                device_id={"level": to_level, "group": ((came_from + 2) % ny) * nz + z},
-                device_id_type=MESH,
-            ).start()
-
     def to_leaf(src, dst, send, recv, other):
         pltpu.make_async_remote_copy(
             src_ref=src,
@@ -348,26 +335,32 @@
         return carry
 
     tiles = (feature // tall) * (labels // tile)
+    def permute_part(n):
+        lax.fori_loop(tiles * n // ny, tiles * (n + 1) // ny, permute, 0)
+
     pick(0)
-    for hop in range(1, ny):
-        up, down = 2 * hop, 2 * hop - 1
-        for which in range(2):
-            wait_for(spread.at[up, half_rows(which)], z_recv.at[up, which])
-            if hop < ny - 1 or which == 0:
-                along_z(up, min(up + 2, nz - 1), which, 1)
-            wait_for(spread.at[down, half_rows(which)], z_recv.at[down, which])
-            if hop < ny - 1 or which == 1:
-                along_z(down, down + 2, which, -1)
-        pick(down)
-        pick(up)
-        lax.fori_loop(tiles * (hop - 1) // ny, tiles * hop // ny, permute, 0)
-        if hop == ny - 1:
-            exchange(0)
-    for which in range(2):
-        wait_for(spread.at[nz - 1, half_rows(which)], z_recv.at[nz - 1, which])
-    pick(nz - 1)
+    for at in (1, 2):
+        from_z(at)
+        pick(at)
+    permute_part(0)
+    from_z(4)
+    along_z(4, 6, 1)
+    along_z(4, 7, 2, 0)
+    from_z(3)
+    along_z(3, 5, -1)
+    along_z(3, 7, -2, 1)
+    pick(3)
+    pick(4)
+    permute_part(1)
+    exchange(0)
+    permute_part(2)
+    for at in (5, 6):
+        from_z(at)
+        pick(at)
     exchange(1)
-    lax.fori_loop(tiles * (ny - 1) // ny, tiles, permute, 0)
+    from_z(7)
+    pick(7)
+    permute_part(3)
 
     pos = pos_ref[...]
     parent_slot, parent_label = pos // labels, (pos % labels).astype(F32)
@@ -586,7 +579,6 @@
             pltpu.VMEM((16 * nz, 128), F32),
             pltpu.VMEM((nz, chunk, 128), BF16),
             pltpu.VMEM((nz, 2, ny, cap // 8, 8, feature // leaves), BF16),
-            pltpu.VMEM((nz, 2, cap // 8, 8, feature // leaves), BF16),
             pltpu.VMEM((leaves, slots // 8, 8, feature // leaves), BF16),
             pltpu.VMEM((ny, leaves, chunk, share), F32),
             pltpu.VMEM((ny, chunk, share), I16),
@@ -607,12 +599,9 @@
             dma,
             dma,
             dma,
-            dma((nz, 2)),
+            dma((nz,)),
             dma,
             dma((ny,)),
-            dma,
-            dma((nz,)),
-            dma,
             dma,
             dma((2, ny)),
             dma,
@@ -625,16 +614,21 @@
             dma,
         ],
         compiler_params=pltpu.CompilerParams(
-            collective_id=0, has_side_effects=True, vmem_limit_bytes=60 << 20
+            collective_id=0, has_side_effects=True, vmem_limit_bytes=52 << 20
         ),
     )(
-        queries,
-        weights[0, 0, 0],
-        block_mask[0, 0, 0],
-        label_map[0, 0],
-        beam_lists[0].T,
-        root_score.T,
-        parent_pos.T,
+        *(
+            pltpu.with_memory_space_constraint(operand, pltpu.HBM)
+            for operand in (
+                queries,
+                weights[0, 0, 0],
+                block_mask[0, 0, 0],
+                label_map[0, 0],
+                beam_lists[0].T,
+                root_score.T,
+                parent_pos.T,
+            )
+        )
     )
     return jnp.transpose(out, (1, 0, 2))[None]
 

time: 76.1 us -> 73.8 us (0.970)
  Pallas kernels: 74 us -> 72.1 us
  local copies, waits for them, and re-layouts: 2 us -> 1 us
    pallas_call x1, Pallas kernels: 74 us -> 72.1 us  [body(): pl.pallas_call(functools.partial(kernel, groups, leaves, cap), out_shape=...]
    broadcast_in_dim x1, local copies, waits for them, and re-layouts: 2 us -> 1 us  [body(): return jnp.transpose(out, (1, 0, 2))[None]]
where the time goes in v5:
time: 73.8 us; the launch traced here: 73.1 us
  Pallas kernels  72.1 us (98%)
  local copies, waits for them, and re-layouts  1 us (1%)
    pallas_call x1, Pallas kernels, body(): pl.pallas_call(functools.partial(kernel, groups, leaves, cap), out_shape=...  72.1 us

profile of v5, /device:TPU:1, one launch (start us, length us, event | category | flops | bytes accessed | tf_op | source)
XLA Modules:
  0.0 73.1 jit_solution(6322323555814642808)
XLA Ops:
  0.0 72.1 %shard_map.73 = f32[4,96,256]{2,1,0:T(8,128)S(1)} custom-call(bf16[96,2048]{1,0:T(8,128)(2,1)} %q_hbm.1, bf16[2048,1024]{1,0:T(8,128)(2,1)} %bitcast.12, s32[16]{0:T(128)} %bitcast.17, s32[1,1024]{1,0:T(1,128)} %bitcast.13, s32[4,96]{1,0:T(4,128)} %bitcast.14, bf16[4,96]{1,0:T(4,128)(2,1)} %bitcast.16, s32[4,96]{1,0:T(4,128)} %bitcast.15), custom_call_target="tpu_custom_call" | custom-call | tf_op jit(solution)/shard_map/pallas_call | solution.py:561
  72.1 1.0 %copy.8 = f32[1,96,4,256]{3,2,1,0:T(4,128)} copy(f32[1,96,4,256]{3,1,2,0:T(8,128)S(1)} %bitcast.11) | data formatting | bytes 786432 | tf_op jit(solution)/shard_map/broadcast_in_dim | solution.py:633

commit v6 on v5

--- a/solution.py
+++ b/solution.py
@@ -165,20 +165,6 @@
     for copy in copies[:2]:
         copy.wait()
     beam = beam_ref[...]
-    group_id = lax.broadcasted_iota(I32, (groups, queries), 0)
-    hit = jnp.zeros((groups, queries), F32)
-    for b in range(beam_len):
-        hit = hit + (beam[b : b + 1, :] == group_id).astype(F32)
-    earlier = (
-        lax.broadcasted_iota(I32, (queries, queries), 0)
-        < lax.broadcasted_iota(I32, (queries, queries), 1)
-    ).astype(F32)
-    rank = jnp.dot(hit.astype(BF16), earlier.astype(BF16), preferred_element_type=F32)
-    place = group_id.astype(F32) * cap + rank
-    slot = [
-        jnp.sum(jnp.where(beam[b : b + 1, :] == group_id, place, 0.0), axis=0, keepdims=True)
-        for b in range(beam_len)
-    ]
     spread[0] = q_ref[:, pl.ds(pl.multiple_of(own_part * part, 128), part)]
     beams_own[...] = jnp.full_like(beams_own, -1)
     beams_own[:beam_len, :queries] = beam
@@ -218,93 +204,26 @@
                     },
                     device_id_type=MESH,
                 ).start()
+
     along_z(0, 2, 1)
     along_z(0, 1, -1)
     along_z(0, 4, 2)
     along_z(0, 3, -2)
 
-    wait_for(beams_in, beam_recv)
-    eight = lax.broadcasted_iota(I32, (8, 128), 0)
-    near_group = jnp.where(eight < ny, eight * nz + z, -2)
-
-    def find_hits(n, carry):
-        names = beams_in[n]
-        found = jnp.zeros((8, 128), F32)
-        for b in range(beam_len):
-            found = found + (names[b : b + 1, :] == near_group).astype(F32)
-        hits[pl.ds(pl.multiple_of(n * 8, 8), 8), :] = found
-        return carry
-
-    lax.fori_loop(0, 2 * nz, find_hits, 0)
-    before = (
-        lax.broadcasted_iota(I32, (128, 128), 0) < lax.broadcasted_iota(I32, (128, 128), 1)
+    group_id = lax.broadcasted_iota(I32, (groups, queries), 0)
+    hit = jnp.zeros((groups, queries), F32)
+    for b in range(beam_len):
+        hit = hit + (beam[b : b + 1, :] == group_id).astype(F32)
+    earlier = (
+        lax.broadcasted_iota(I32, (queries, queries), 0)
+        < lax.broadcasted_iota(I32, (queries, queries), 1)
     ).astype(F32)
-    hits[...] = jnp.dot(
-        hits[...].astype(BF16), before.astype(BF16), preferred_element_type=F32
-    )
-    near_slot = lax.broadcasted_iota(I32, (ny * cap, 128), 0).astype(F32)
-
-    def make_select(n, carry):
-        names = beams_in[n]
-        place = eight.astype(F32) * cap + hits[pl.ds(pl.multiple_of(n * 8, 8), 8), :] + 1.0
-        chosen = jnp.zeros((ny * cap, 128), F32)
-        for b in range(beam_len):
-            at = jnp.sum(
-                jnp.where(names[b : b + 1, :] == near_group, place, 0.0), axis=0, keepdims=True
-            )
-            chosen = chosen + (at - 1.0 == near_slot).astype(F32)
-        select[n % nz, pl.ds(pl.multiple_of((n // nz) * ny * cap, 16), ny * cap), :] = chosen.astype(
-            BF16
-        )
-        return carry
-
-    lax.fori_loop(0, 2 * nz, make_select, 0)
-
-    blocks = cap // 8
-
-    def slot_blocks(group):
-        return pl.ds(group * blocks, blocks)
-
-    def chunk_blocks(step):
-        return pl.ds(step * (chunk // 8), chunk // 8)
-
-    def distance_blocks(at):
-        return pl.ds(at * (half // 8), half // 8)
-
-    def pick(at):
-        rows = jnp.dot(select[at, :, :queries], spread[at], preferred_element_type=F32)
-        picked[at] = rows.astype(BF16).reshape(2, ny, blocks, 8, part)
-        pltpu.make_async_copy(
-            picked.at[at, level, y], rows_in.at[own_part, slot_blocks(at * ny + y)], y_recv.at[at // 2]
-        ).start()
-        for flip, step in ((0, 2), (1, 2), (0, 1), (0, 3), (1, 1), (1, 3), (1, 0)):
-            to_level, to_row = (level + flip) % 2, (y + step) % ny
-            pltpu.make_async_remote_copy(
-                src_ref=picked.at[at, to_level, to_row],
-                dst_ref=rows_in.at[own_part, slot_blocks(at * ny + y)],
-                send_sem=y_send,
-                recv_sem=y_recv.at[at // 2],
-                device_id={"level": to_level, "group": to_row * nz + z},
-                device_id_type=MESH,
-            ).start()
-
-    def to_leaf(src, dst, send, recv, other):
-        pltpu.make_async_remote_copy(
-            src_ref=src,
-            dst_ref=dst,
-            send_sem=send,
-            recv_sem=recv,
-            device_id={"leaf": other},
-            device_id_type=MESH,
-        ).start()
-
-    def exchange(c):
-        two = pl.ds(fetched, 2)
-        wait_for(rows_in.at[two, chunk_blocks(c)], y_recv.at[c])
-        for n, other in enumerate((right, left)):
-            rows = rows_in.at[two, distance_blocks(2 * c + n)]
-            to_leaf(rows, rows, fwd_send, fwd_recv.at[n, c], other)
-
+    rank = jnp.dot(hit.astype(BF16), earlier.astype(BF16), preferred_element_type=F32)
+    place = group_id.astype(F32) * cap + rank
+    slot = [
+        jnp.sum(jnp.where(beam[b : b + 1, :] == group_id, place, 0.0), axis=0, keepdims=True)
+        for b in range(beam_len)
+    ]
     for copy in copies[2:]:
         copy.wait()
     tile, tall = 256, 1024
@@ -338,29 +257,7 @@
     def permute_part(n):
         lax.fori_loop(tiles * n // ny, tiles * (n + 1) // ny, permute, 0)
 
-    pick(0)
-    for at in (1, 2):
-        from_z(at)
-        pick(at)
     permute_part(0)
-    from_z(4)
-    along_z(4, 6, 1)
-    along_z(4, 7, 2, 0)
-    from_z(3)
-    along_z(3, 5, -1)
-    along_z(3, 7, -2, 1)
-    pick(3)
-    pick(4)
-    permute_part(1)
-    exchange(0)
-    permute_part(2)
-    for at in (5, 6):
-        from_z(at)
-        pick(at)
-    exchange(1)
-    from_z(7)
-    pick(7)
-    permute_part(3)
 
     pos = pos_ref[...]
     parent_slot, parent_label = pos // labels, (pos % labels).astype(F32)
@@ -384,6 +281,111 @@
         choose[b * queries : (b + 1) * queries, :] = (
             (columns[:queries, b : b + 1] == across_slots).astype(F32).astype(BF16)
         )
+
+    wait_for(beams_in, beam_recv)
+    eight = lax.broadcasted_iota(I32, (8, 128), 0)
+    near_group = jnp.where(eight < ny, eight * nz + z, -2)
+
+    def find_hits(n, carry):
+        names = beams_in[n]
+        found = jnp.zeros((8, 128), F32)
+        for b in range(beam_len):
+            found = found + (names[b : b + 1, :] == near_group).astype(F32)
+        hits[pl.ds(pl.multiple_of(n * 8, 8), 8), :] = found
+        return carry
+
+    lax.fori_loop(0, 2 * nz, find_hits, 0)
+    before = (
+        lax.broadcasted_iota(I32, (128, 128), 0) < lax.broadcasted_iota(I32, (128, 128), 1)
+    ).astype(F32)
+    hits[...] = jnp.dot(
+        hits[...].astype(BF16), before.astype(BF16), preferred_element_type=F32
+    )
+    near_slot = lax.broadcasted_iota(I32, (ny * cap, 128), 0).astype(F32)
+
+    def make_select(n, carry):
+        names = beams_in[n]
+        place = eight.astype(F32) * cap + hits[pl.ds(pl.multiple_of(n * 8, 8), 8), :] + 1.0
+        chosen = jnp.zeros((ny * cap, 128), F32)
+        for b in range(beam_len):
+            at = jnp.sum(
+                jnp.where(names[b : b + 1, :] == near_group, place, 0.0), axis=0, keepdims=True
+            )
+            chosen = chosen + (at - 1.0 == near_slot).astype(F32)
+        select[n % nz, pl.ds(pl.multiple_of((n // nz) * ny * cap, 16), ny * cap), :] = chosen.astype(
+            BF16
+        )
+        return carry
+
+    lax.fori_loop(0, 2 * nz, make_select, 0)
+
+    blocks = cap // 8
+
+    def slot_blocks(group):
+        return pl.ds(group * blocks, blocks)
+
+    def chunk_blocks(step):
+        return pl.ds(step * (chunk // 8), chunk // 8)
+
+    def distance_blocks(at):
+        return pl.ds(at * (half // 8), half // 8)
+
+    def pick(at):
+        rows = jnp.dot(select[at, :, :queries], spread[at], preferred_element_type=F32)
+        picked[at] = rows.astype(BF16).reshape(2, ny, blocks, 8, part)
+        pltpu.make_async_copy(
+            picked.at[at, level, y], rows_in.at[own_part, slot_blocks(at * ny + y)], y_recv.at[at // 2]
+        ).start()
+        for flip, step in ((0, 1), (0, 3), (1, 1), (1, 3), (1, 0), (0, 2), (1, 2)):
+            to_level, to_row = (level + flip) % 2, (y + step) % ny
+            pltpu.make_async_remote_copy(
+                src_ref=picked.at[at, to_level, to_row],
+                dst_ref=rows_in.at[own_part, slot_blocks(at * ny + y)],
+                send_sem=y_send,
+                recv_sem=y_recv.at[at // 2],
+                device_id={"level": to_level, "group": to_row * nz + z},
+                device_id_type=MESH,
+            ).start()
+
+    def to_leaf(src, dst, send, recv, other):
+        pltpu.make_async_remote_copy(
+            src_ref=src,
+            dst_ref=dst,
+            send_sem=send,
+            recv_sem=recv,
+            device_id={"leaf": other},
+            device_id_type=MESH,
+        ).start()
+
+    def exchange(c):
+        two = pl.ds(fetched, 2)
+        wait_for(rows_in.at[two, chunk_blocks(c)], y_recv.at[c])
+        for n, other in enumerate((right, left)):
+            rows = rows_in.at[two, distance_blocks(2 * c + n)]
+            to_leaf(rows, rows, fwd_send, fwd_recv.at[n, c], other)
+
+    pick(0)
+    for at in (1, 2):
+        from_z(at)
+        pick(at)
+    from_z(4)
+    along_z(4, 6, 1)
+    along_z(4, 7, 2, 0)
+    from_z(3)
+    along_z(3, 5, -1)
+    along_z(3, 7, -2, 1)
+    pick(3)
+    pick(4)
+    permute_part(1)
+    exchange(0)
+    permute_part(2)
+    for at in (5, 6):
+        from_z(at)
+        pick(at)
+    exchange(1)
+    from_z(7)
+    pick(7)
+    permute_part(3)
 
     def stage(t, carry):
         @pl.when(t < 2)

time: 73.8 us -> 73.1 us (level)
  no operation moved by 1% of the time
where the time goes in v6:
time: 73.1 us; the launch traced here: 73 us
  Pallas kernels  72 us (98%)
  local copies, waits for them, and re-layouts  1 us (1%)
    pallas_call x1, Pallas kernels, body(): pl.pallas_call(functools.partial(kernel, groups, leaves, cap), out_shape=...  72 us

profile of v6, /device:TPU:1, one launch (start us, length us, event | category | flops | bytes accessed | tf_op | source)
XLA Modules:
  0.0 73.0 jit_solution(10195250354283124565)
XLA Ops:
  0.0 72.0 %shard_map.73 = f32[4,96,256]{2,1,0:T(8,128)S(1)} custom-call(bf16[96,2048]{1,0:T(8,128)(2,1)} %q_hbm.1, bf16[2048,1024]{1,0:T(8,128)(2,1)} %bitcast.12, s32[16]{0:T(128)} %bitcast.17, s32[1,1024]{1,0:T(1,128)} %bitcast.13, s32[4,96]{1,0:T(4,128)} %bitcast.14, bf16[4,96]{1,0:T(4,128)(2,1)} %bitcast.16, s32[4,96]{1,0:T(4,128)} %bitcast.15), custom_call_target="tpu_custom_call" | custom-call | tf_op jit(solution)/shard_map/pallas_call | solution.py:563
  72.0 1.0 %copy.8 = f32[1,96,4,256]{3,2,1,0:T(4,128)} copy(f32[1,96,4,256]{3,1,2,0:T(8,128)S(1)} %bitcast.11) | data formatting | bytes 786432 | tf_op jit(solution)/shard_map/broadcast_in_dim | solution.py:635

commit v7 on v6

--- a/solution.py
+++ b/solution.py
@@ -226,7 +226,7 @@
     ]
     for copy in copies[2:]:
         copy.wait()
-    tile, tall = 256, 1024
+    tile, tall = 256, 2048
     mask_rows = feature // mask_ref.shape[0]
 
     def fill_perm(n, carry):

time: 73.1 us -> 73.1 us (level)
  no operation moved by 1% of the time
where the time goes in v7:
time: 73.1 us; the launch traced here: 73 us
  Pallas kernels  72 us (98%)
  local copies, waits for them, and re-layouts  1 us (1%)
    pallas_call x1, Pallas kernels, body(): pl.pallas_call(functools.partial(kernel, groups, leaves, cap), out_shape=...  72 us

profile of v7, /device:TPU:1, one launch (start us, length us, event | category | flops | bytes accessed | tf_op | source)
XLA Modules:
  0.0 73.0 jit_solution(15975713066508225998)
XLA Ops:
  0.0 72.0 %shard_map.73 = f32[4,96,256]{2,1,0:T(8,128)S(1)} custom-call(bf16[96,2048]{1,0:T(8,128)(2,1)} %q_hbm.1, bf16[2048,1024]{1,0:T(8,128)(2,1)} %bitcast.12, s32[16]{0:T(128)} %bitcast.17, s32[1,1024]{1,0:T(1,128)} %bitcast.13, s32[4,96]{1,0:T(4,128)} %bitcast.14, bf16[4,96]{1,0:T(4,128)(2,1)} %bitcast.16, s32[4,96]{1,0:T(4,128)} %bitcast.15), custom_call_target="tpu_custom_call" | custom-call | tf_op jit(solution)/shard_map/pallas_call | solution.py:563
  72.0 1.0 %copy.8 = f32[1,96,4,256]{3,2,1,0:T(4,128)} copy(f32[1,96,4,256]{3,1,2,0:T(8,128)S(1)} %bitcast.11) | data formatting | bytes 786432 | tf_op jit(solution)/shard_map/broadcast_in_dim | solution.py:635
